TPU v7x, 128 devices: a whole 4x4x4 slice. The times are simulated.
128 devices in a mesh: gx: 16 (over z, y), gy: 8 (over x, core).
Axes of the slice: x: 4, y: 4, z: 4, core: 2. Of those that a mesh axis runs over, the one named last changes fastest.
Arguments:
- features: bfloat16 [262144, 512], P(('gx', 'gy')), may hold values from -6 to 6
- point_block: int32 [262144], P(('gx', 'gy')), may hold values from 0 to 15, as said below
- block_count: int32 [128], P(('gx', 'gy')), may hold values from 1 to 16, as said below
- z_dest_dev: int32 [128, 16], P(('gx', 'gy')), may hold values from 0 to 15, as said below
- z_dest_slot: int32 [128, 16], P(('gx', 'gy')), may hold values from 0 to 7
- z_back_owner: int32 [128, 8], P(('gx', 'gy')), may hold values from 0 to 15, as said below
- z_back_block: int32 [128, 8], P(('gx', 'gy')), may hold values from 0 to 15, as said below
- hil_dest_dev: int32 [128, 8], P(('gx', 'gy')), may hold values from 0 to 7, as said below
- hil_dest_slot: int32 [128, 8], P(('gx', 'gy')), may hold values from 0 to 7
- hil_back_dev: int32 [128, 8], P(('gx', 'gy')), may hold values from 0 to 7, as said below
- hil_back_slot: int32 [128, 8], P(('gx', 'gy')), may hold values from 0 to 7, as said below
- norm_gain: float32 [2, 2, 512], replicated, may hold values from 0.5 to 1.5
- w_qkv: bfloat16 [2, 512, 1536], replicated
- w_out: bfloat16 [2, 512, 512], replicated, may hold values from -0.25 to 0.25
- w_up: bfloat16 [2, 512, 2048], replicated, may hold values from -0.25 to 0.25
- w_down: bfloat16 [2, 2048, 512], replicated, may hold values from -0.125 to 0.125
Outputs:
- returned: bfloat16 [262144, 512], P(('gx', 'gy'))
Inputs may be any that keep to these rules, and one draw needn't show every extreme that they name: `point_block`: on each owner every id below its block_count names exactly 128 rows; rows with ids at or above it are dead. `block_count`: along each gx line of owners (one gy index) the counts sum to 128, and some owner of every line holds 16 blocks. `z_dest_dev`: along each gx line the live blocks fill every (device, slot) exactly once; at most 1 live blocks of one owner go to one device, a bound reached in every line; entries of dead blocks are arbitrary. `z_back_owner`: the inverse of z_dest_dev and z_dest_slot on live blocks. `z_back_block`: the inverse of z_dest_dev and z_dest_slot on live blocks. `hil_dest_dev`: along each gy line the slots are permuted among devices; every device sends exactly 2 blocks to each device it sends to. `hil_back_dev`: the inverse of hil_dest_dev and hil_dest_slot. `hil_back_slot`: the inverse of hil_dest_dev and hil_dest_slot.
All inputs are finite; a program needn't handle non-finite values.
Results may differ from a plain program's by a relative error of at most 0.023.
The roundings to bfloat16 on the way count: a program that leaves them out, or rounds other values in their place, can miss the bound.
Values may be sent and summed in bfloat16 or wider, within the bound.
A program may use at most 128 MiB of HBM per device.

v0:
```python
import jax
import jax.numpy as jnp
from jax import lax
from jax.sharding import PartitionSpec as P

HEADS = 8
PATCH = 1024


EPSILON = 1e-05


def normed(values_in, gain_row):
    centered = values_in - jnp.mean(values_in, axis=-1, keepdims=True)
    variance = jnp.mean(centered * centered, axis=-1, keepdims=True)
    return centered * lax.rsqrt(variance + EPSILON) * gain_row


def layer_patch(patch_rows, gain_pair, weight_qkv, weight_out, weight_up, weight_down):
    row_count, feature_width = patch_rows.shape
    head_size = feature_width // HEADS
    residual = patch_rows.astype(jnp.float32)
    normal_in = normed(residual, gain_pair[0]).astype(jnp.bfloat16)
    joined = jnp.dot(normal_in, weight_qkv, preferred_element_type=jnp.float32).astype(jnp.bfloat16)
    queries = joined[:, :feature_width].reshape(row_count, HEADS, head_size)
    keys_all = joined[:, feature_width : 2 * feature_width].reshape(row_count, HEADS, head_size)
    values_all = joined[:, 2 * feature_width :].reshape(row_count, HEADS, head_size)
    query_step = min(512, row_count)
    scaling = head_size ** (-0.5)

    def attend(query_block):
        scores = (
            jnp.einsum("qhd,khd->hqk", query_block, keys_all, preferred_element_type=jnp.float32)
            * scaling
        )
        highest = jnp.max(scores, axis=-1, keepdims=True)
        exponent = jnp.exp(scores - highest)
        weights = (exponent / jnp.sum(exponent, axis=-1, keepdims=True)).astype(jnp.bfloat16)
        mixed = jnp.einsum("hqk,khd->qhd", weights, values_all, preferred_element_type=jnp.float32)
        return mixed.astype(jnp.bfloat16)

    attended = lax.map(
        attend, queries.reshape(row_count // query_step, query_step, HEADS, head_size)
    )
    attended = attended.reshape(row_count, feature_width)
    after_attention = (
        residual + jnp.dot(attended, weight_out, preferred_element_type=jnp.float32)
    ).astype(jnp.bfloat16)
    middle = after_attention.astype(jnp.float32)
    normal_mid = normed(middle, gain_pair[1]).astype(jnp.bfloat16)
    hidden = jax.nn.gelu(jnp.dot(normal_mid, weight_up, preferred_element_type=jnp.float32)).astype(
        jnp.bfloat16
    )
    return (middle + jnp.dot(hidden, weight_down, preferred_element_type=jnp.float32)).astype(
        jnp.bfloat16
    )


def rank_within(groups, order_key):
    same = groups[:, None] == groups[None, :]
    before = order_key[None, :] < order_key[:, None]
    return jnp.sum((same & before).astype(jnp.int32), axis=1)


def pack_lanes(rows_in, lane_keys, lane_count):
    picker = (lane_keys[None, :] == jnp.arange(lane_count, dtype=jnp.int32)[:, None]).astype(
        jnp.bfloat16
    )
    return jnp.dot(picker, rows_in, preferred_element_type=jnp.float32).astype(jnp.bfloat16)


def read_lanes(arrived, lane_keys):
    picker = (lane_keys[:, None] == jnp.arange(arrived.shape[0], dtype=jnp.int32)[None, :]).astype(
        jnp.bfloat16
    )
    return jnp.dot(picker, arrived, preferred_element_type=jnp.float32).astype(jnp.bfloat16)


def shards(
    features,
    point_block,
    block_count,
    z_dest_dev,
    z_dest_slot,
    z_back_owner,
    z_back_block,
    hil_dest_dev,
    hil_dest_slot,
    hil_back_dev,
    hil_back_slot,
    norm_gain,
    w_qkv,
    w_out,
    w_up,
    w_down,
):
    row_count, feature_width = features.shape
    capacity = z_dest_dev.shape[1]
    blocks_held = z_back_owner.shape[1]
    block_rows = row_count // capacity
    line_x = lax.axis_size("gx")
    line_y = lax.axis_size("gy")
    positions = jnp.arange(row_count, dtype=jnp.int32)
    ordering = jnp.argsort(point_block * row_count + positions)
    packed = features[ordering].reshape(capacity, block_rows * feature_width)
    block_ids = jnp.arange(capacity, dtype=jnp.int32)
    alive = block_ids < block_count[0]
    owner_dest = jnp.where(alive, z_dest_dev[0], -1)
    slot_ids = jnp.arange(blocks_held, dtype=jnp.int32)
    lane_width = max(1, capacity // line_x)
    owner_keys = jnp.where(alive, owner_dest * lane_width + rank_within(owner_dest, block_ids), -1)
    patch_keys = z_back_owner[0] * lane_width + rank_within(z_back_owner[0], z_back_block[0])
    outbox = pack_lanes(packed, owner_keys, line_x * lane_width).reshape(line_x, lane_width, -1)
    arrived = lax.all_to_all(outbox, "gx", split_axis=0, concat_axis=0, tiled=True)
    current = read_lanes(arrived.reshape(line_x * lane_width, -1), patch_keys)

    def run_layer(blocks_now, layer_index):
        patches = blocks_now.reshape(-1, PATCH, feature_width)

        def single(patch_rows):
            return layer_patch(
                patch_rows,
                norm_gain[layer_index],
                w_qkv[layer_index],
                w_out[layer_index],
                w_up[layer_index],
                w_down[layer_index],
            )

        return lax.map(single, patches).reshape(blocks_held, block_rows * feature_width)

    current = run_layer(current, 0)
    pair_y = blocks_held // 4
    send_keys = hil_dest_dev[0] * pair_y + rank_within(hil_dest_dev[0], slot_ids)
    recv_keys = hil_back_dev[0] * pair_y + rank_within(hil_back_dev[0], hil_back_slot[0])
    outbox = pack_lanes(current, send_keys, line_y * pair_y).reshape(line_y, pair_y, -1)
    arrived = lax.all_to_all(outbox, "gy", split_axis=0, concat_axis=0, tiled=True)
    current = read_lanes(arrived.reshape(line_y * pair_y, -1), recv_keys)
    current = run_layer(current, 1)
    outbox = pack_lanes(current, recv_keys, line_y * pair_y).reshape(line_y, pair_y, -1)
    arrived = lax.all_to_all(outbox, "gy", split_axis=0, concat_axis=0, tiled=True)
    current = read_lanes(arrived.reshape(line_y * pair_y, -1), send_keys)
    outbox = pack_lanes(current, patch_keys, line_x * lane_width).reshape(line_x, lane_width, -1)
    arrived = lax.all_to_all(outbox, "gx", split_axis=0, concat_axis=0, tiled=True)
    at_home = read_lanes(arrived.reshape(line_x * lane_width, -1), owner_keys)
    restored = (
        jnp.zeros((row_count, feature_width), jnp.bfloat16)
        .at[ordering]
        .set(at_home.reshape(row_count, feature_width))
    )
    return restored


def solution(mesh):
    in_specs = (
        P(("gx", "gy"), None),
        P(("gx", "gy")),
        P(("gx", "gy")),
        P(("gx", "gy"), None),
        P(("gx", "gy"), None),
        P(("gx", "gy"), None),
        P(("gx", "gy"), None),
        P(("gx", "gy"), None),
        P(("gx", "gy"), None),
        P(("gx", "gy"), None),
        P(("gx", "gy"), None),
        P(),
        P(),
        P(),
        P(),
        P(),
    )
    out_specs = P(("gx", "gy"), None)
    return jax.shard_map(shards, mesh=mesh, in_specs=in_specs, out_specs=out_specs, check_vma=False)
```

profile of v0, /device:TPU:1, one launch (start us, length us, event | category | flops | bytes accessed | tf_op | source)
XLA Modules:
  0.0 358.5 jit_solution(4592900584559137932)
XLA Ops:
  8.5 9.2 %gather_fusion = bf16[2048,512]{1,0:T(8,128)(2,1)} fusion(bf16[2048,512]{1,0:T(8,128)(2,1)S(1)} %copy-done, s32[2048]{0:T(1024)S(1)} %get-tuple-element.195), kind=kCustom, calls=%fused_computation | custom fusion | bytes 4202496 | tf_op jit(solution)/shard_map/gather | solution.py:105
  29.8 8.9 %all-to-all-start = ((bf16[16,2,32768]{2,1,0:T(2,128)(2,1)}), bf16[16,2,32768]{2,1,0:T(2,128)(2,1)S(1)}, u32[]{:S(2)}, u32[]{:S(2)}) async-start(bf16[16,2,32768]{2,1,0:T(2,128)(2,1)} %reshape.274), calls=%async_computation | async-start | bytes 4194304 | tf_op jit(solution)/shard_map/all_to_all | solution.py:114
  39.9 29.8 %all-to-all-done = bf16[16,2,32768]{2,1,0:T(2,128)(2,1)S(1)} async-done(((bf16[16,2,32768]{2,1,0:T(2,128)(2,1)}), bf16[16,2,32768]{2,1,0:T(2,128)(2,1)S(1)}, u32[]{:S(2)}, u32[]{:S(2)}) %all-to-all-start) | async-done | bytes 2097184 | tf_op jit(solution)/shard_map/all_to_all | solution.py:114
  69.7 6.8 %reshape.275 = bf16[16,1,65536]{2,1,0:T(2,128)(2,1)} reshape(bf16[16,2,32768]{2,1,0:T(2,128)(2,1)S(1)} %all-to-all-done) | data formatting | bytes 4194304
  76.5 5.9 %fusion.57 = f32[8,65536]{1,0:T(8,128)} fusion(bf16[16,1,65536]{2,1,0:T(2,128)(2,1)} %reshape.275, s32[8]{0:T(128)S(1)} %bitcast_add_fusion.4), kind=kOutput, calls=%fused_computation.51 | convolution fusion | flops 17825920 | bytes 4194336 | tf_op jit(solution)/shard_map/dot_general | solution.py:76
  100.7 34.3 %while.34 = (s32[]{:T(128)}, bf16[2,512,8,64]{1,3,2,0:T(8,128)(2,1)S(1)}, bf16[2,512,8,64]{1,3,2,0:T(8,128)(2,1)S(1)}, bf16[1024,8,64]{0,2,1:T(8,128)(2,1)S(1)}, bf16[1024,8,64]{0,2,1:T(8,128)(2,1)}, /*index=5*/s32[]{:T(128)}) while((s32[]{:T(128)}, bf16[2,512,8,64]{1,3,2,0:T(8,128)(2,1)S(1)}, bf16[2,512,8,64]{1,3,2,0:T(8,128)(2,1)S(1)}, ...), condition=%wide.region_10.11_spmd, body=%wide.region_7.0_spmd.sunk | while | flops 1094976512 | bytes 36733004 | solution.py:42
  101.1 8.2 %fusion.215 = (f32[8,512]{1,0:T(8,128)S(1)}, f32[8,512,1024]{2,1,0:T(8,128)}) fusion(bf16[1024,8,64]{0,2,1:T(8,128)(2,1)S(1)} %get-tuple-element.290, bf16[2,512,8,64]{1,3,2,0:T(8,128)(2,1)S(1)} %get-tuple-element.289, s32[]{:T(128)} %get-tuple-element.281), kind=kOutput, calls=%fused_computation.191.clone.1 | convolution fusion | flops 549454848 | bytes 18366468 | tf_op jit(solution)/shard_map/while/body/eval_jaxpr/while/body/eval_jaxpr/sub | solution.py:37
  109.3 8.7 %fusion.216 = bf16[2,512,8,64]{1,3,2,0:T(8,128)(2,1)S(1)} fusion(bf16[2,512,8,64]{1,3,2,0:T(8,128)(2,1)S(1)} %get-tuple-element.282, s32[]{:T(128)} %get-tuple-element.281, bf16[1024,8,64]{0,2,1:T(8,128)(2,1)} %get-tuple-element.291, f32[8,512,1024]{2,1,0:T(8,128)} %get-tuple-element.266, f32[8,512]{1,0:T(8,128)S(1)} %get-tuple-element.267), kind=kOutput, calls=%fused_computation.12.clone.1 | convolution fusion | flops 545521664 | bytes 18366468 | tf_op jit(solution)/shard_map/while/body/eval_jaxpr/while/body/eval_jaxpr/hqk,khd->qhd/dot_general | solution.py:39
  118.0 8.2 %fusion.215 = (f32[8,512]{1,0:T(8,128)S(1)}, f32[8,512,1024]{2,1,0:T(8,128)}) fusion(bf16[1024,8,64]{0,2,1:T(8,128)(2,1)S(1)} %get-tuple-element.290, bf16[2,512,8,64]{1,3,2,0:T(8,128)(2,1)S(1)} %get-tuple-element.289, s32[]{:T(128)} %get-tuple-element.281), kind=kOutput, calls=%fused_computation.191.clone.1 | convolution fusion | flops 549454848 | bytes 18366468 | tf_op jit(solution)/shard_map/while/body/eval_jaxpr/while/body/eval_jaxpr/sub | solution.py:37
  126.3 8.7 %fusion.216 = bf16[2,512,8,64]{1,3,2,0:T(8,128)(2,1)S(1)} fusion(bf16[2,512,8,64]{1,3,2,0:T(8,128)(2,1)S(1)} %get-tuple-element.282, s32[]{:T(128)} %get-tuple-element.281, bf16[1024,8,64]{0,2,1:T(8,128)(2,1)} %get-tuple-element.291, f32[8,512,1024]{2,1,0:T(8,128)} %get-tuple-element.266, f32[8,512]{1,0:T(8,128)S(1)} %get-tuple-element.267), kind=kOutput, calls=%fused_computation.12.clone.1 | convolution fusion | flops 545521664 | bytes 18366468 | tf_op jit(solution)/shard_map/while/body/eval_jaxpr/while/body/eval_jaxpr/hqk,khd->qhd/dot_general | solution.py:39
  138.0 7.7 %fusion.88 = bf16[1024,512]{0,1:T(8,128)(2,1)S(1)} fusion(bf16[1024,512]{0,1:T(8,128)(2,1)S(1)} %get-tuple-element.202, bf16[2,2048,512]{2,1,0:T(8,128)(2,1)} %param.33, bf16[2,512,2048]{2,1,0:T(8,128)(2,1)} %param.32, f32[512]{0:T(512)S(1)} %bitcast.217, f32[1024]{0:T(1024)S(1)} %add_rsqrt_fusion.1, f32[1024]{0:T(1024)S(1)} %broadcast_multiply_fusion.2), kind=kOutput, calls=%fused_computation.90 | convolution fusion | flops 4318035968 | bytes 7350272 | tf_op jit(solution)/shard_map/while/body/eval_jaxpr/dot_general | solution.py:54
  149.7 6.4 %all-to-all-start.1 = ((bf16[8,2,65536]{2,1,0:T(2,128)(2,1)}), bf16[8,2,65536]{2,1,0:T(2,128)(2,1)}, u32[]{:S(2)}, u32[]{:S(2)}) async-start(bf16[8,2,65536]{2,1,0:T(2,128)(2,1)} %reshape.238), calls=%async_computation.1 | async-start | bytes 4194304 | tf_op jit(solution)/shard_map/all_to_all | solution.py:137
  156.4 25.9 %all-to-all-done.1 = bf16[8,2,65536]{2,1,0:T(2,128)(2,1)} async-done(((bf16[8,2,65536]{2,1,0:T(2,128)(2,1)}), bf16[8,2,65536]{2,1,0:T(2,128)(2,1)}, u32[]{:S(2)}, u32[]{:S(2)}) %all-to-all-start.1) | async-done | bytes 2097184 | tf_op jit(solution)/shard_map/all_to_all | solution.py:137
  204.5 34.1 %while.35 = (s32[]{:T(128)}, bf16[2,512,8,64]{1,3,2,0:T(8,128)(2,1)S(1)}, bf16[2,512,8,64]{1,3,2,0:T(8,128)(2,1)S(1)}, bf16[1024,8,64]{0,2,1:T(8,128)(2,1)S(1)}, bf16[1024,8,64]{0,2,1:T(8,128)(2,1)}, /*index=5*/s32[]{:T(128)}) while((s32[]{:T(128)}, bf16[2,512,8,64]{1,3,2,0:T(8,128)(2,1)S(1)}, bf16[2,512,8,64]{1,3,2,0:T(8,128)(2,1)S(1)}, ...), condition=%wide.region_18.19_spmd, body=%wide.region_15.18_spmd.sunk | while | flops 1094976512 | bytes 36733004 | solution.py:42
  204.5 8.2 %fusion.220 = (f32[8,512]{1,0:T(8,128)S(1)}, f32[8,512,1024]{2,1,0:T(8,128)}) fusion(bf16[1024,8,64]{0,2,1:T(8,128)(2,1)S(1)} %get-tuple-element.308, bf16[2,512,8,64]{1,3,2,0:T(8,128)(2,1)S(1)} %get-tuple-element.307, s32[]{:T(128)} %get-tuple-element.299), kind=kOutput, calls=%fused_computation.192.clone.1 | convolution fusion | flops 549454848 | bytes 18366468 | tf_op jit(solution)/shard_map/while/body/eval_jaxpr/while/body/eval_jaxpr/sub | solution.py:37
  212.7 8.7 %fusion.221 = bf16[2,512,8,64]{1,3,2,0:T(8,128)(2,1)S(1)} fusion(bf16[2,512,8,64]{1,3,2,0:T(8,128)(2,1)S(1)} %get-tuple-element.300, s32[]{:T(128)} %get-tuple-element.299, bf16[1024,8,64]{0,2,1:T(8,128)(2,1)} %get-tuple-element.309, f32[8,512,1024]{2,1,0:T(8,128)} %get-tuple-element.273, f32[8,512]{1,0:T(8,128)S(1)} %get-tuple-element.274), kind=kOutput, calls=%fused_computation.31.clone.1 | convolution fusion | flops 545521664 | bytes 18366468 | tf_op jit(solution)/shard_map/while/body/eval_jaxpr/while/body/eval_jaxpr/hqk,khd->qhd/dot_general | solution.py:39
  221.5 8.2 %fusion.220 = (f32[8,512]{1,0:T(8,128)S(1)}, f32[8,512,1024]{2,1,0:T(8,128)}) fusion(bf16[1024,8,64]{0,2,1:T(8,128)(2,1)S(1)} %get-tuple-element.308, bf16[2,512,8,64]{1,3,2,0:T(8,128)(2,1)S(1)} %get-tuple-element.307, s32[]{:T(128)} %get-tuple-element.299), kind=kOutput, calls=%fused_computation.192.clone.1 | convolution fusion | flops 549454848 | bytes 18366468 | tf_op jit(solution)/shard_map/while/body/eval_jaxpr/while/body/eval_jaxpr/sub | solution.py:37
  229.7 8.7 %fusion.221 = bf16[2,512,8,64]{1,3,2,0:T(8,128)(2,1)S(1)} fusion(bf16[2,512,8,64]{1,3,2,0:T(8,128)(2,1)S(1)} %get-tuple-element.300, s32[]{:T(128)} %get-tuple-element.299, bf16[1024,8,64]{0,2,1:T(8,128)(2,1)} %get-tuple-element.309, f32[8,512,1024]{2,1,0:T(8,128)} %get-tuple-element.273, f32[8,512]{1,0:T(8,128)S(1)} %get-tuple-element.274), kind=kOutput, calls=%fused_computation.31.clone.1 | convolution fusion | flops 545521664 | bytes 18366468 | tf_op jit(solution)/shard_map/while/body/eval_jaxpr/while/body/eval_jaxpr/hqk,khd->qhd/dot_general | solution.py:39
  241.6 7.7 %fusion.89 = bf16[1024,512]{0,1:T(8,128)(2,1)S(1)} fusion(bf16[1024,512]{0,1:T(8,128)(2,1)S(1)} %get-tuple-element.204, bf16[2,2048,512]{2,1,0:T(8,128)(2,1)} %param.33, bf16[2,512,2048]{2,1,0:T(8,128)(2,1)} %param.32, f32[512]{0:T(512)S(1)} %bitcast.216, f32[1024]{0:T(1024)S(1)} %add_rsqrt_fusion, f32[1024]{0:T(1024)S(1)} %broadcast_multiply_fusion), kind=kOutput, calls=%fused_computation.91 | convolution fusion | flops 4318035968 | bytes 7350272 | tf_op jit(solution)/shard_map/while/body/eval_jaxpr/dot_general | solution.py:54
  258.3 26.1 %all-to-all-done.2 = bf16[8,2,65536]{2,1,0:T(2,128)(2,1)S(1)} async-done(((bf16[8,2,65536]{2,1,0:T(2,128)(2,1)}), bf16[8,2,65536]{2,1,0:T(2,128)(2,1)S(1)}, u32[]{:S(2)}, u32[]{:S(2)}) %all-to-all-start.2) | async-done | bytes 2097184 | tf_op jit(solution)/shard_map/all_to_all | solution.py:141
  299.6 30.9 %all-to-all-done.3 = bf16[16,2,32768]{2,1,0:T(2,128)(2,1)S(1)} async-done(((bf16[16,2,32768]{2,1,0:T(2,128)(2,1)}), bf16[16,2,32768]{2,1,0:T(2,128)(2,1)S(1)}, u32[]{:S(2)}, u32[]{:S(2)}) %all-to-all-start.3) | async-done | bytes 2097184 | tf_op jit(solution)/shard_map/all_to_all | solution.py:144
  330.5 6.8 %reshape.277 = bf16[16,1,65536]{2,1,0:T(2,128)(2,1)} reshape(bf16[16,2,32768]{2,1,0:T(2,128)(2,1)S(1)} %all-to-all-done.3) | data formatting | bytes 4194304
  337.3 5.9 %convolution_convert_fusion = bf16[16,65536]{1,0:T(8,128)(2,1)} fusion(bf16[16,1,65536]{2,1,0:T(2,128)(2,1)} %reshape.277, s32[16]{0:T(128)S(1)} %compare_select_fusion.3), kind=kOutput, calls=%fused_computation.40 | convolution fusion | flops 34603264 | bytes 4194368 | tf_op jit(solution)/shard_map/dot_general | solution.py:76
  346.6 11.5 %scatter_custom_fusion = bf16[2048,512]{1,0:T(8,128)(2,1)} fusion(s32[2048]{0:T(1024)} %get-tuple-element.196, bf16[2048,512]{1,0:T(8,128)(2,1)} %reshape.264, bf16[]{:T(256)} %constant.91.clone.1), kind=kCustom, calls=%fused_computation.122 | custom fusion | bytes 2097664 | tf_op jit(solution)/shard_map/scatter | solution.py:149
  (155 shorter events, 98.8 us)
Async XLA Ops:
  0.0 8.5 %copy-start = (bf16[2048,512]{1,0:T(8,128)(2,1)S(1)}, bf16[2048,512]{1,0:T(8,128)(2,1)}, u32[]{:S(2)}) copy-start(bf16[2048,512]{1,0:T(8,128)(2,1)} %param.20) | copy-start | bytes 6291460
  17.7 2.9 copy-start.19
  29.8 9.0 %copy-start.13 = (f32[2,2,512]{2,1,0:T(2,128)S(1)}, f32[2,2,512]{2,1,0:T(2,128)}, u32[]{:S(2)}) copy-start(f32[2,2,512]{2,1,0:T(2,128)} %param.29) | copy-start | bytes 24580
  29.8 9.7 %copy-start.26 = (s32[1,8]{1,0:T(1,128)S(1)}, s32[1,8]{1,0:T(1,128)}, u32[]{:S(2)}) copy-start(s32[1,8]{1,0:T(1,128)} %param.26) | copy-start | bytes 100
  29.8 9.9 %copy-start.14 = (s32[1,8]{1,0:T(1,128)S(1)}, s32[1,8]{1,0:T(1,128)}, u32[]{:S(2)}) copy-start(s32[1,8]{1,0:T(1,128)} %param.25) | copy-start | bytes 100
  29.8 9.9 %copy-start.17 = (s32[1,8]{1,0:T(1,128)S(1)}, s32[1,8]{1,0:T(1,128)}, u32[]{:S(2)}) copy-start(s32[1,8]{1,0:T(1,128)} %param.24) | copy-start | bytes 100
  29.8 39.9 %all-to-all-start = ((bf16[16,2,32768]{2,1,0:T(2,128)(2,1)}), bf16[16,2,32768]{2,1,0:T(2,128)(2,1)S(1)}, u32[]{:S(2)}, u32[]{:S(2)}) async-start(bf16[16,2,32768]{2,1,0:T(2,128)(2,1)} %reshape.274), calls=%async_computation | async-start | bytes 4194304 | tf_op jit(solution)/shard_map/all_to_all | solution.py:114
  39.6 36.8 %copy-start.28 = (s32[8]{0:T(128)}, s32[8]{0:T(128)S(1)}, u32[]{:S(2)}) copy-start(s32[8]{0:T(128)S(1)} %convert_reduce_fusion.4) | copy-start | bytes 100
  39.9 36.6 %copy-start.24 = (s32[8]{0:T(128)}, s32[8]{0:T(128)S(1)}, u32[]{:S(2)}) copy-start(s32[8]{0:T(128)S(1)} %convert_reduce_fusion.5) | copy-start | bytes 100
  95.5 3.8 %copy-start.6 = (bf16[1024,512]{1,0:T(8,128)(2,1)S(1)}, bf16[1024,512]{1,0:T(8,128)(2,1)}, u32[]{:S(2)}) copy-start(bf16[1024,512]{1,0:T(8,128)(2,1)} %get-tuple-element.188) | copy-start | bytes 3145732
  149.7 6.4 %copy-start.12 = (f32[1,1,512]{2,1,0:T(1,128)S(1)}, f32[1,1,512]{2,1,0:T(1,128)}, u32[]{:S(2)}) copy-start(f32[1,1,512]{2,1,0:T(1,128)} %get-tuple-element.194) | copy-start | bytes 6148
  149.7 6.5 %copy-start.15 = (s32[1,8]{1,0:T(1,128)S(1)}, s32[1,8]{1,0:T(1,128)}, u32[]{:S(2)}) copy-start(s32[1,8]{1,0:T(1,128)} %param.28) | copy-start | bytes 100
  149.7 6.6 %copy-start.16 = (s32[1,8]{1,0:T(1,128)S(1)}, s32[1,8]{1,0:T(1,128)}, u32[]{:S(2)}) copy-start(s32[1,8]{1,0:T(1,128)} %param.27) | copy-start | bytes 100
  149.7 32.7 %all-to-all-start.1 = ((bf16[8,2,65536]{2,1,0:T(2,128)(2,1)}), bf16[8,2,65536]{2,1,0:T(2,128)(2,1)}, u32[]{:S(2)}, u32[]{:S(2)}) async-start(bf16[8,2,65536]{2,1,0:T(2,128)(2,1)} %reshape.238), calls=%async_computation.1 | async-start | bytes 4194304 | tf_op jit(solution)/shard_map/all_to_all | solution.py:137
  199.3 3.8 %copy-start.7 = (bf16[1024,512]{1,0:T(8,128)(2,1)S(1)}, bf16[1024,512]{1,0:T(8,128)(2,1)}, u32[]{:S(2)}) copy-start(bf16[1024,512]{1,0:T(8,128)(2,1)} %get-tuple-element.185) | copy-start | bytes 3145732
  253.3 4.9 %copy-start.18 = (s32[1,8]{1,0:T(1,128)S(1)}, s32[1,8]{1,0:T(1,128)}, u32[]{:S(2)}) copy-start(s32[1,8]{1,0:T(1,128)} %param.24) | copy-start | bytes 100
  253.3 4.9 %copy-start.25 = (s32[8]{0:T(128)S(1)}, s32[8]{0:T(128)}, u32[]{:S(2)}) copy-start(s32[8]{0:T(128)} %copy-done.24) | copy-start | bytes 100
  253.3 4.9 %copy-start.27 = (s32[1,8]{1,0:T(1,128)S(1)}, s32[1,8]{1,0:T(1,128)}, u32[]{:S(2)}) copy-start(s32[1,8]{1,0:T(1,128)} %param.26) | copy-start | bytes 100
  253.3 5.0 %copy-start.29 = (s32[8]{0:T(128)S(1)}, s32[8]{0:T(128)}, u32[]{:S(2)}) copy-start(s32[8]{0:T(128)} %copy-done.28) | copy-start | bytes 100
  253.3 31.1 %all-to-all-start.2 = ((bf16[8,2,65536]{2,1,0:T(2,128)(2,1)}), bf16[8,2,65536]{2,1,0:T(2,128)(2,1)S(1)}, u32[]{:S(2)}, u32[]{:S(2)}) async-start(bf16[8,2,65536]{2,1,0:T(2,128)(2,1)} %reshape.245), calls=%async_computation.2 | async-start | bytes 4194304 | tf_op jit(solution)/shard_map/all_to_all | solution.py:141
  295.7 3.9 %copy-start.20 = (s32[1,16]{1,0:T(1,128)S(1)}, s32[1,16]{1,0:T(1,128)}, u32[]{:S(2)}) copy-start(s32[1,16]{1,0:T(1,128)} %param.23) | copy-start | bytes 196
  295.7 3.9 %copy-start.22 = (s32[16]{0:T(128)S(1)}, s32[16]{0:T(128)}, u32[]{:S(2)}) copy-start(s32[16]{0:T(128)} %copy-done.21) | copy-start | bytes 196
  295.7 34.8 %all-to-all-start.3 = ((bf16[16,2,32768]{2,1,0:T(2,128)(2,1)}), bf16[16,2,32768]{2,1,0:T(2,128)(2,1)S(1)}, u32[]{:S(2)}, u32[]{:S(2)}) async-start(bf16[16,2,32768]{2,1,0:T(2,128)(2,1)} %reshape.276), calls=%async_computation.3 | async-start | bytes 4194304 | tf_op jit(solution)/shard_map/all_to_all | solution.py:144
  343.2 14.9 %copy-start.1 = (bf16[2048,512]{1,0:T(8,128)(2,1)S(1)}, bf16[2048,512]{1,0:T(8,128)(2,1)}, u32[]{:S(2)}) copy-start(bf16[2048,512]{1,0:T(8,128)(2,1)} %param.20) | copy-start | bytes 6291460
  (10 other events, 14.6 us)
where the time goes:
time: 364 us; the launch traced here: 359 us
  waiting for transfers between devices  113 us (31%)
  matrix products  111 us (30%)
  local copies, waits for them, and re-layouts  90.5 us (25%)
  starting transfers between devices  24.1 us (7%)
  other arithmetic  17.9 us (5%)
    all_to_all x2, waiting for transfers between devices, shards(): lax.all_to_all(outbox, 'gx', split_axis=0, concat_axis=0, tiled=True)  60.7 us
    all_to_all x2, waiting for transfers between devices, shards(): lax.all_to_all(outbox, 'gy', split_axis=0, concat_axis=0, tiled=True)  52 us
    dot_general x4, matrix products, attend(): jnp.einsum('hqk,khd->qhd', weights, values_all, preferred_element_type=jn...  34.9 us
    sub x4, matrix products, attend(): exponent = jnp.exp(scores - highest)  32.8 us
    unnamed x70, local copies, waits for them, and re-layouts  24.9 us
    dot_general x2, matrix products, layer_patch(): jnp.dot(hidden, weight_down, preferred_element_type=jnp.float32)  15.3 us
    dot_general x3, matrix products, read_lanes(): jnp.dot(picker, arrived, preferred_element_type=jnp.float32)  13.6 us
    all_to_all x2, starting transfers between devices, shards(): lax.all_to_all(outbox, 'gx', split_axis=0, concat_axis=0, tiled=True)  12.8 us
  transfers between devices with their start and end apart: 4, of which 4 were waited for; matrix products, arithmetic and copies ran while one was open for 0% of the time, Pallas kernels for 0%

commit v1 on v0

v1 whole, which is shorter than its diff:
```python
import functools

import jax
import jax.numpy as jnp
from jax import lax
from jax.experimental import pallas as pl
from jax.experimental.pallas import tpu as pltpu
from jax.sharding import PartitionSpec as P

MESH = pl.DeviceIdType.MESH
D = 512
FF = 2048
BLOCK = 128
CAP = 16
SLOTS = 8
ROWS = CAP * BLOCK
CHUNKS = 4
STEP = BLOCK // CHUNKS
PART = SLOTS * STEP
LANES = 16
PAIRS = 4
EPSILON = 1e-05
BF = jnp.bfloat16
F32 = jnp.float32
SEND_SLOT, RECV_LANE, BACK_SLOT, HOME_LANE, FROM_LANE, OWN_BLOCK = 0, 16, 24, 40, 56, 64

GX_OFFSETS = (
    (0, 1), (1, 0), (0, 3), (3, 0), (1, 1), (3, 3), (1, 3), (3, 1),
    (2, 0), (0, 2), (2, 1), (1, 2), (2, 3), (3, 2), (2, 2),
)
GY_OFFSETS = ((1, 0), (3, 0), (2, 0), (1, 1), (3, 1), (2, 1), (0, 1))


def normed(values_in, gain_row):
    centered = values_in - jnp.mean(values_in, axis=-1, keepdims=True)
    variance = jnp.mean(centered * centered, axis=-1, keepdims=True)
    return centered * lax.rsqrt(variance + EPSILON) * gain_row


def gelu(x):
    inner = x * (0.7978845608028654 + 0.035677408136300125 * (x * x))
    return (0.5 * x) * (1.0 + jnp.tanh(inner))


def row_keys(blocks_of):
    groups = blocks_of.shape[0]
    masks = [jnp.where(blocks_of == b, 1.0, 0.0) for b in range(CAP)]
    stacked = jnp.concatenate(masks, axis=0)
    stacked_low = stacked.astype(BF)
    row = lax.broadcasted_iota(jnp.int32, (128, 128), 0)
    col = lax.broadcasted_iota(jnp.int32, (128, 128), 1)
    before = jnp.where(row < col, 1.0, 0.0).astype(BF)
    within = jnp.dot(stacked_low, before, preferred_element_type=F32)
    totals = jnp.dot(stacked_low, jnp.ones((128, 128), BF), preferred_element_type=F32).astype(BF)
    size = CAP * groups
    high = lax.broadcasted_iota(jnp.int32, (size, size), 0)
    low = lax.broadcasted_iota(jnp.int32, (size, size), 1)
    earlier = jnp.where((high // groups == low // groups) & (low < high), 1.0, 0.0).astype(BF)
    ahead = jnp.dot(earlier, totals, preferred_element_type=F32)
    ranks = within + ahead
    total = jnp.zeros((groups, 128), F32)
    for b in range(CAP):
        part = slice(b * groups, (b + 1) * groups)
        total = total + stacked[part] * (ranks[part] + float(b * BLOCK))
    return total


def kernel(
    table, blocks_ref, gain_ref, feat_h, wqkv_h, wout_h, wup_h, wdown_h, out_ref,
    feat, wqkv, wout, wup, wdown, keys, lanes_a, keys_wide, xs, q_s, k_s, v_s, y_s, lanes_1, lanes_2, lanes_b, arr_b,
    ax0, ax1, ax2, ax3, ay0, ay1, ay2, ay3, az0, az1, az2, az3,
    local_sem, send_a, recv_a, send_1, recv_1, send_2, recv_2, send_b, recv_b,
):
    arr_x = (ax0, ax1, ax2, ax3)
    arr_1 = (ay0, ay1, ay2, ay3)
    arr_2 = (az0, az1, az2, az3)
    gx = lax.axis_index("gx")
    gy = lax.axis_index("gy")
    z, y = gx // 4, gx % 4
    x, core = gy // 2, gy % 2
    gx_peers = [((z + dz) % 4) * 4 + (y + dy) % 4 for dz, dy in GX_OFFSETS]
    gx_sources = [((z + 4 - dz) % 4) * 4 + (y + 4 - dy) % 4 for dz, dy in GX_OFFSETS]
    gy_peers = [((x + dx) % 4) * 2 + (core + dc) % 2 for dx, dc in GY_OFFSETS]
    gy_sources = [((x + 4 - dx) % 4) * 2 + (core + dc) % 2 for dx, dc in GY_OFFSETS]

    loads = [pltpu.make_async_copy(feat_h, feat, local_sem.at[0])]
    for layer in range(2):
        for i, (src, dst) in enumerate(((wqkv_h, wqkv), (wout_h, wout), (wup_h, wup), (wdown_h, wdown))):
            loads.append(pltpu.make_async_copy(src.at[layer], dst.at[layer], local_sem.at[1 + layer * 4 + i]))
    for load in loads:
        load.start()

    barrier = pltpu.get_barrier_semaphore()
    for peer in gx_peers:
        pl.semaphore_signal(barrier, inc=1, device_id=(peer, gy), device_id_type=MESH)
    for peer in gy_peers:
        pl.semaphore_signal(barrier, inc=1, device_id=(gx, peer), device_id_type=MESH)

    def gx_copy(lanes, c, arrived, send, recv, peer, source):
        return pltpu.make_async_remote_copy(
            src_ref=lanes.at[c, peer], dst_ref=arrived.at[source],
            send_sem=send.at[c, peer], recv_sem=recv.at[c, source],
            device_id=(peer, gy), device_id_type=MESH,
        )

    def gy_copy(lanes, c, arrived, send, recv, peer, source):
        return pltpu.make_async_remote_copy(
            src_ref=lanes.at[c, pl.ds(peer * 2, 2)], dst_ref=arrived.at[pl.ds(source * 2, 2)],
            send_sem=send.at[c, peer], recv_sem=recv.at[c, source],
            device_id=(gx, peer), device_id_type=MESH,
        )

    key_rows = row_keys(blocks_ref[...])
    keys[...] = key_rows.astype(jnp.int32)
    padded = jnp.concatenate([key_rows, jnp.zeros((128 - 16, 128), F32)], axis=0)
    turned = padded.T.astype(jnp.int32)
    for g in range(16):
        keys_wide[g * 128 : (g + 1) * 128, :] = jnp.broadcast_to(turned[:, g : g + 1], (128, 128))

    loads[0].wait()
    for c in range(CHUNKS):
        for half in range(2):
            rows_in = lax.broadcasted_iota(jnp.int32, (STEP, 128), 0) + c * STEP
            wanted = jnp.concatenate(
                [rows_in + table[OWN_BLOCK + half * 8 + k] for k in range(8)], axis=0
            )
            picker = jnp.concatenate(
                [jnp.where(wanted == keys[g : g + 1, :], 1.0, 0.0).astype(BF) for g in range(16)], axis=1
            )
            packed = jnp.dot(picker, feat[...], preferred_element_type=F32).astype(BF)
            lanes_a[c, half * 8 : half * 8 + 8] = packed.reshape(8, STEP, D)
        if c == 0:
            pl.semaphore_wait(barrier, len(gx_peers) + len(gy_peers))
        for peer in gx_peers:
            gx_copy(lanes_a, c, arr_x[c], send_a, recv_a, peer, gx).start()
        arr_x[c][gx] = lanes_a[c, gx]

    lane_of = lax.broadcasted_iota(jnp.int32, (PART, 128), 1)
    low_half = lane_of < 64

    def project(layer, c):
        values = xs[c].astype(F32)
        normal = normed(values, gain_ref[layer, 0:1, :]).astype(BF)
        joined = jnp.dot(normal, wqkv[layer], preferred_element_type=F32)
        rows = pl.ds(c * PART, PART)
        for pair in range(PAIRS):
            q_s[pair, rows, :] = joined[:, pair * 128 : (pair + 1) * 128].astype(BF) * jnp.asarray(0.125, BF)
            k_s[pair, rows, :] = joined[:, D + pair * 128 : D + (pair + 1) * 128].astype(BF)
            v_s[pair, rows, 0:128] = joined[:, 2 * D + pair * 128 : 2 * D + (pair + 1) * 128].astype(BF)
            v_s[pair, rows, 128:256] = jnp.ones((PART, 128), BF)

    def finish(layer, c):
        rows = pl.ds(c * PART, PART)
        mixed = []
        for pair in range(PAIRS):
            q_pair = q_s[pair, rows, :]
            zero = jnp.zeros_like(q_pair)
            both = []
            for head in range(2):
                q_head = jnp.where(low_half, q_pair, zero) if head == 0 else jnp.where(low_half, zero, q_pair)
                scores = lax.dot_general(q_head, k_s[pair], (((1,), (1,)), ((), ())), preferred_element_type=F32)
                highest = jnp.max(scores, axis=-1, keepdims=True)
                weights = jnp.exp(scores - highest).astype(BF)
                summed = jnp.dot(weights, v_s[pair], preferred_element_type=F32)
                both.append(summed[:, 0:128] / summed[:, 128:256])
            mixed.append(jnp.where(low_half, both[0], both[1]).astype(BF))
        attended = jnp.concatenate(mixed, axis=1)
        after = (xs[c].astype(F32) + jnp.dot(attended, wout[layer], preferred_element_type=F32)).astype(BF)
        middle = after.astype(F32)
        normal = normed(middle, gain_ref[layer, 1:2, :]).astype(BF)
        total = middle
        for j in range(4):
            cols = slice(j * 512, (j + 1) * 512)
            hidden = gelu(jnp.dot(normal, wup[layer, :, cols], preferred_element_type=F32)).astype(BF)
            total = total + jnp.dot(hidden, wdown[layer, cols, :], preferred_element_type=F32)
        y_s[...] = total.astype(BF).reshape(SLOTS, STEP, D)

    def receive_and_project(layer, first, arrived, waits):
        def step(c, carry):
            for i in range(CHUNKS):
                @pl.when(c == i)
                def _():
                    waits(i)
                    for slot in range(SLOTS):
                        xs[i, slot * STEP : (slot + 1) * STEP, :] = arrived[i][table[first + slot]]
            project(layer, c)
            return carry
        lax.fori_loop(0, CHUNKS, step, 0)

    def wait_x(i):
        for source in gx_sources:
            gx_copy(lanes_a, i, arr_x[i], send_a, recv_a, source, source).wait_recv()

    loads[1].wait()
    receive_and_project(0, FROM_LANE, arr_x, wait_x)
    for load in loads[2:5]:
        load.wait()

    def compute_and_send(layer, first, lanes, arrived, send, recv, after):
        def step(c, carry):
            finish(layer, c)
            for lane in range(LANES):
                lanes[c, lane] = y_s[table[first + lane]]
            for i in range(CHUNKS):
                @pl.when(c == i)
                def _():
                    for peer in gy_peers:
                        gy_copy(lanes, i, arrived[i], send, recv, peer, gy).start()
                    for p in range(2):
                        arrived[i][gy * 2 + p] = lanes[i, gy * 2 + p]
                    after(i)
            return carry
        lax.fori_loop(0, CHUNKS, step, 0)

    compute_and_send(0, SEND_SLOT, lanes_1, arr_1, send_1, recv_1, lambda i: None)

    def wait_1(i):
        for source in gy_sources:
            gy_copy(lanes_1, i, arr_1[i], send_1, recv_1, source, source).wait_recv()

    loads[5].wait()
    receive_and_project(1, RECV_LANE, arr_1, wait_1)
    for load in loads[6:]:
        load.wait()

    def forward(i):
        for source in gy_sources:
            gy_copy(lanes_2, i, arr_2[i], send_2, recv_2, source, source).wait_recv()
        for k in range(LANES):
            lanes_b[i, k] = arr_2[i][table[HOME_LANE + k]]
        for peer in gx_peers:
            gx_copy(lanes_b, i, arr_b.at[i], send_b, recv_b, peer, gx).start()
        arr_b[i, gx] = lanes_b[i, gx]

    def after_2(i):
        if i >= 2:
            forward(i - 2)

    compute_and_send(1, BACK_SLOT, lanes_2, arr_2, send_2, recv_2, after_2)
    forward(2)

    quarter = lax.broadcasted_iota(jnp.int32, (1, 128), 1)

    def unpack(c, carry):
        for source in gx_sources:
            gx_copy(lanes_b, c, arr_b.at[c], send_b, recv_b, source, source).wait_recv()
        wanted = []
        for j in range(4):
            owned = [table[OWN_BLOCK + 4 * j + k] + c * STEP - STEP * k for k in range(4)]
            chosen = jnp.where(
                quarter < 2 * STEP,
                jnp.where(quarter < STEP, owned[0], owned[1]),
                jnp.where(quarter < 3 * STEP, owned[2], owned[3]),
            )
            wanted.append(chosen + quarter)
        landed = arr_b[c].reshape(LANES * STEP, D)
        for tile in range(4):
            rows = slice(tile * 512, (tile + 1) * 512)
            wide = keys_wide[rows, :]
            picker = jnp.concatenate([jnp.where(wide == w, 1.0, 0.0).astype(BF) for w in wanted], axis=1)
            part = jnp.dot(picker, landed, preferred_element_type=F32).astype(BF)

            @pl.when(c == 0)
            def _():
                out_ref[rows, :] = part

            @pl.when(c > 0)
            def _():
                out_ref[rows, :] = out_ref[rows, :] + part

        @pl.when(c == 0)
        def _():
            forward(3)
        return carry

    lax.fori_loop(0, CHUNKS, unpack, 0)

    for c in range(CHUNKS):
        for peer in gx_peers:
            gx_copy(lanes_a, c, arr_x[c], send_a, recv_a, peer, gx).wait_send()
            gx_copy(lanes_b, c, arr_b.at[c], send_b, recv_b, peer, gx).wait_send()
        for peer in gy_peers:
            gy_copy(lanes_1, c, arr_1[c], send_1, recv_1, peer, gy).wait_send()
            gy_copy(lanes_2, c, arr_2[c], send_2, recv_2, peer, gy).wait_send()


def rank_within(groups, order_key):
    same = groups[:, None] == groups[None, :]
    before = order_key[None, :] < order_key[:, None]
    return jnp.sum((same & before).astype(jnp.int32), axis=1)


def shards(
    features, point_block, block_count, z_dest_dev, z_dest_slot, z_back_owner, z_back_block,
    hil_dest_dev, hil_dest_slot, hil_back_dev, hil_back_slot, norm_gain, w_qkv, w_out, w_up, w_down,
):
    lanes = jnp.arange(LANES, dtype=jnp.int32)
    slots = jnp.arange(SLOTS, dtype=jnp.int32)
    alive = lanes < block_count[0]
    send_keys = hil_dest_dev[0] * 2 + rank_within(hil_dest_dev[0], slots)
    recv_keys = hil_back_dev[0] * 2 + rank_within(hil_back_dev[0], hil_back_slot[0])

    def placed(keys, values):
        hit = keys[None, :] == lanes[:, None]
        return jnp.sum(jnp.where(hit, values[None, :], 0), axis=1)

    owned = placed(jnp.where(alive, z_dest_dev[0], -1), lanes * BLOCK + 1000000) - 1000000
    table = jnp.concatenate(
        [
            placed(send_keys, slots),
            recv_keys,
            placed(recv_keys, slots),
            placed(z_back_owner[0], send_keys),
            z_back_owner[0],
            owned,
        ]
    ).astype(jnp.int32)

    any_space = pl.BlockSpec(memory_space=pl.ANY)
    vmem = pl.BlockSpec(memory_space=pltpu.VMEM)
    dma = pltpu.SemaphoreType.DMA
    landing = [pltpu.VMEM((LANES, STEP, D), BF) for _ in range(3 * CHUNKS)]
    return pl.pallas_call(
        kernel,
        out_shape=jax.ShapeDtypeStruct((ROWS, D), BF),
        in_specs=[pl.BlockSpec(memory_space=pltpu.SMEM), vmem, vmem] + [any_space] * 5,
        out_specs=vmem,
        scratch_shapes=[
            pltpu.VMEM((ROWS, D), BF),
            pltpu.VMEM((2, D, 3 * D), BF),
            pltpu.VMEM((2, D, D), BF),
            pltpu.VMEM((2, D, FF), BF),
            pltpu.VMEM((2, FF, D), BF),
            pltpu.VMEM((16, 128), jnp.int32),
            pltpu.VMEM((CHUNKS, LANES, STEP, D), BF),
            pltpu.VMEM((ROWS, 128), jnp.int32),
            pltpu.VMEM((CHUNKS, PART, D), BF),
            pltpu.VMEM((PAIRS, CHUNKS * PART, 128), BF),
            pltpu.VMEM((PAIRS, CHUNKS * PART, 128), BF),
            pltpu.VMEM((PAIRS, CHUNKS * PART, 256), BF),
            pltpu.VMEM((SLOTS, STEP, D), BF),
            pltpu.VMEM((CHUNKS, LANES, STEP, D), BF),
            pltpu.VMEM((CHUNKS, LANES, STEP, D), BF),
            pltpu.VMEM((CHUNKS, LANES, STEP, D), BF),
            pltpu.VMEM((CHUNKS, LANES, STEP, D), BF),
        ]
        + landing
        + [
            dma((9,)),
            dma((CHUNKS, 16)), dma((CHUNKS, 16)), dma((CHUNKS, 8)), dma((CHUNKS, 8)),
            dma((CHUNKS, 8)), dma((CHUNKS, 8)), dma((CHUNKS, 16)), dma((CHUNKS, 16)),
        ],
        compiler_params=pltpu.CompilerParams(
            collective_id=0, has_side_effects=True, vmem_limit_bytes=63 * 1024 * 1024
        ),
    )(table, point_block.reshape(16, 128), norm_gain, features, w_qkv, w_out, w_up, w_down)


def solution(mesh):
    split = P(("gx", "gy"), None)
    flat = P(("gx", "gy"))
    in_specs = (split, flat, flat) + (split,) * 8 + (P(),) * 5
    return jax.shard_map(shards, mesh=mesh, in_specs=in_specs, out_specs=split, check_vma=False)
```

time: 364 us -> 125 us (0.34); the launches traced: 359 us -> 125 us
  Pallas kernels: 0 us -> 114 us
  waiting for transfers between devices: 113 us -> 0 us
  matrix products: 111 us -> 0 us
  local copies, waits for them, and re-layouts: 90.5 us -> 4.3 us
  starting transfers between devices: 24.1 us -> 0 us
  other arithmetic: 17.9 us -> 5.34 us
    pallas_call x0 -> x1, Pallas kernels: none -> 114 us  [shards(): pl.pallas_call(kernel, out_shape=jax.ShapeDtypeStruct((ROWS, D), BF), in_...]
    all_to_all x4 -> x0, waiting for transfers between devices: 113 us -> none  [the longest x2 60.7 us: shards(): lax.all_to_all(outbox, 'gx', split_axis=0, concat_axis=0, tiled=True)]
    dot_general x17 -> x0, matrix products: 77.7 us -> none  [the longest x4 34.9 us: attend(): jnp.einsum('hqk,khd->qhd', weights, values_all, preferred_element_type=jn...]
    sub x4 -> x0, matrix products: 32.8 us -> none  [attend(): exponent = jnp.exp(scores - highest)]
    all_to_all x4 -> x0, starting transfers between devices: 24.1 us -> none  [the longest x2 12.8 us: shards(): lax.all_to_all(outbox, 'gx', split_axis=0, concat_axis=0, tiled=True)]
    unnamed x70 -> x1, local copies, waits for them, and re-layouts: 24.9 us -> 3.05 us
    reshape x11 -> x0, local copies, waits for them, and re-layouts: 17.7 us -> none  [the longest x1 3.37 us: shards(): at_home.reshape(row_count, feature_width)]
    scatter x1 -> x0, local copies, waits for them, and re-layouts: 11.5 us -> none  [shards(): restored = jnp.zeros((row_count, feature_width), jnp.bfloat16).at[orderin...]
  transfers between devices with their start and end apart: 4 -> 0, of which waited for: 4 -> 0; matrix products, arithmetic and copies ran while one was open for 0% -> 0% of each run, Pallas kernels for 0% -> 0%
where the time goes in v1:
time: 125 us
  Pallas kernels  114 us (91%)
  other arithmetic  5.34 us (4%)
  local copies, waits for them, and re-layouts  4.3 us (3%)
    pallas_call x1, Pallas kernels, shards(): pl.pallas_call(kernel, out_shape=jax.ShapeDtypeStruct((ROWS, D), BF), in_...  114 us
    unnamed x1, local copies, waits for them, and re-layouts  3.05 us

profile of v1, /device:TPU:1, one launch (start us, length us, event | category | flops | bytes accessed | tf_op | source)
XLA Modules:
  0.0 124.8 jit_solution(2543359283292974640)
XLA Ops:
  0.7 0.7 fusion.1
  1.3 0.9 convert_reduce_fusion
  2.2 0.7 fusion.2
  2.9 0.7 multiply_add_fusion.1
  3.5 0.9 convert_reduce_fusion.1
  4.5 0.7 fusion.3
  5.1 0.1 select_reduce_fusion
  5.2 0.7 select_reduce_fusion.1
  6.0 1.3 %concatenate.3.table = s32[80]{0:T(128)} concatenate(s32[16]{0:T(128)S(1)} %get-tuple-element.6, s32[8]{0:T(128)S(1)} %multiply_add_fusion.1, s32[16]{0:T(128)S(1)} %get-tuple-element.7, s32[16]{0:T(128)S(1)} %get-tuple-element.5, s32[8]{0:T(128)} %bitcast.26, s32[16]{0:T(128)S(1)} %broadcast_add_fusion), dimensions={0} | concatenate | bytes 640 | tf_op jit(solution)/shard_map/concatenate | solution.py:308
  7.2 114.5 %shard_map.127 = bf16[2048,512]{1,0:T(8,128)(2,1)} custom-call(s32[80]{0:T(128)} %concatenate.3.table, s32[16,128]{1,0:T(8,128)} %bitcast.22, f32[2,2,512]{2,1,0:T(2,128)} %gain_ref.1, bf16[2048,512]{1,0:T(8,128)(2,1)} %feat_h.1, bf16[2,512,1536]{2,1,0:T(8,128)(2,1)} %wqkv_h.1, bf16[2,512,512]{2,1,0:T(8,128)(2,1)} %wout_h.1, bf16[2,512,2048]{2,1,0:T(8,128)(2,1)} %wup_h.1, ...), custom_call_target="tpu_custom_call" | custom-call | tf_op jit(solution)/shard_map/pallas_call | solution.py:323
  121.7 3.0 %copy.16 = bf16[2048,512]{1,0:T(8,128)(2,1)} copy(bf16[2048,512]{1,0:T(8,128)(2,1)} %shard_map.127) | data formatting | bytes 4194304
  (2 shorter events, 0.0 us)

commit v2 on v1

v2 whole, which is shorter than its diff:
```python
import contextlib

import jax
import jax.numpy as jnp
from jax import lax
from jax.experimental import pallas as pl
from jax.experimental.pallas import tpu as pltpu
from jax.sharding import PartitionSpec as P

MESH = pl.DeviceIdType.MESH


def scope(name):
    return contextlib.nullcontext()


D = 512
FF = 2048
BLOCK = 128
CAP = 16
SLOTS = 8
ROWS = CAP * BLOCK
CHUNKS = 4
STEP = BLOCK // CHUNKS
PART = SLOTS * STEP
FINE = 8
FINE_STEP = BLOCK // FINE
LANES = 16
PAIRS = 4
EPSILON = 1e-05
BF = jnp.bfloat16
F32 = jnp.float32
SEND_SLOT, RECV_LANE, BACK_SLOT, HOME_LANE, FROM_LANE, OWN_BLOCK = 0, 16, 24, 40, 56, 64
NOWHERE = -1000000

GX_OFFSETS = (
    (0, 1), (1, 0), (0, 3), (3, 0), (1, 1), (3, 3), (1, 3), (3, 1),
    (2, 0), (0, 2), (2, 1), (1, 2), (2, 3), (3, 2), (2, 2),
)
GY_OFFSETS = ((1, 0), (3, 0), (2, 0), (1, 1), (3, 1), (2, 1), (0, 1))


def normed(values_in, gain_row):
    centered = values_in - jnp.mean(values_in, axis=-1, keepdims=True)
    variance = jnp.mean(centered * centered, axis=-1, keepdims=True)
    return centered * lax.rsqrt(variance + EPSILON) * gain_row


def gelu(x):
    inner = x * (0.7978845608028654 + 0.035677408136300125 * (x * x))
    return (0.5 * x) * (1.0 + jnp.tanh(inner))


def row_keys(blocks_of):
    groups = blocks_of.shape[0]
    masks = [jnp.where(blocks_of == b, 1.0, 0.0) for b in range(CAP)]
    stacked = jnp.concatenate(masks, axis=0)
    stacked_low = stacked.astype(BF)
    row = lax.broadcasted_iota(jnp.int32, (128, 128), 0)
    col = lax.broadcasted_iota(jnp.int32, (128, 128), 1)
    before = jnp.where(row < col, 1.0, 0.0).astype(BF)
    within = jnp.dot(stacked_low, before, preferred_element_type=F32)
    totals = jnp.dot(stacked_low, jnp.ones((128, 128), BF), preferred_element_type=F32).astype(BF)
    size = CAP * groups
    high = lax.broadcasted_iota(jnp.int32, (size, size), 0)
    low = lax.broadcasted_iota(jnp.int32, (size, size), 1)
    earlier = jnp.where((high // groups == low // groups) & (low < high), 1.0, 0.0).astype(BF)
    ahead = jnp.dot(earlier, totals, preferred_element_type=F32)
    ranks = within + ahead
    total = jnp.zeros((groups, 128), F32)
    for b in range(CAP):
        part = slice(b * groups, (b + 1) * groups)
        total = total + stacked[part] * (ranks[part] + float(b * BLOCK))
    return total


def own_table(table, counts, z_dest):
    dests = [jnp.where(b < counts[0], z_dest[0, b], -1) for b in range(CAP)]
    for lane in range(LANES):
        chosen = jnp.int32(NOWHERE)
        for b in range(CAP):
            chosen = jnp.where(dests[b] == lane, b * BLOCK, chosen)
        table[OWN_BLOCK + lane] = chosen


def move_tables(table, z_owner, h_dest, h_back, h_slot):
    dest = [h_dest[0, s] for s in range(SLOTS)]
    back = [h_back[0, s] for s in range(SLOTS)]
    slot = [h_slot[0, s] for s in range(SLOTS)]
    owner = [z_owner[0, s] for s in range(SLOTS)]
    send_keys = []
    recv_keys = []
    for s in range(SLOTS):
        key = dest[s] * 2
        for other in range(s):
            key = key + jnp.where(dest[other] == dest[s], 1, 0)
        send_keys.append(key)
        key = back[s] * 2
        for other in range(SLOTS):
            if other != s:
                key = key + jnp.where((back[other] == back[s]) & (slot[other] < slot[s]), 1, 0)
        recv_keys.append(key)
        table[RECV_LANE + s] = key
        table[FROM_LANE + s] = owner[s]
    for lane in range(LANES):
        send = jnp.int32(0)
        back_slot = jnp.int32(0)
        home = jnp.int32(0)
        for s in range(SLOTS):
            send = jnp.where(send_keys[s] == lane, s, send)
            back_slot = jnp.where(recv_keys[s] == lane, s, back_slot)
            home = jnp.where(owner[s] == lane, send_keys[s], home)
        table[SEND_SLOT + lane] = send
        table[BACK_SLOT + lane] = back_slot
        table[HOME_LANE + lane] = home


def kernel(
    counts, z_dest, z_owner, h_dest, h_back, h_slot,
    blocks_ref, gain_ref, feat_h, wqkv_h, wout_h, wup_h, wdown_h, out_ref,
    table, feat, wqkv, wout, wup, wdown, keys, lanes_a, keys_wide, xs, q_s, k_s, v_s, mid_s, y_s, lanes_1, lanes_2, lanes_b, arr_b,
    *rest,
):
    arr_x, arr_1, arr_2 = rest[:CHUNKS], rest[CHUNKS : CHUNKS + FINE], rest[CHUNKS + FINE : CHUNKS + 2 * FINE]
    local_sem, send_a, recv_a, send_1, recv_1, send_2, recv_2, send_b, recv_b = rest[CHUNKS + 2 * FINE :]
    gx = lax.axis_index("gx")
    gy = lax.axis_index("gy")
    z, y = gx // 4, gx % 4
    x, core = gy // 2, gy % 2
    gx_peers = [((z + dz) % 4) * 4 + (y + dy) % 4 for dz, dy in GX_OFFSETS]
    gy_peers = [((x + dx) % 4) * 2 + (core + dc) % 2 for dx, dc in GY_OFFSETS]

    loads = [pltpu.make_async_copy(feat_h, feat, local_sem.at[0])]
    for layer in range(2):
        for i, (src, dst) in enumerate(((wqkv_h, wqkv), (wout_h, wout), (wup_h, wup), (wdown_h, wdown))):
            loads.append(pltpu.make_async_copy(src.at[layer], dst.at[layer], local_sem.at[1 + layer * 4 + i]))
    for load in loads:
        load.start()

    barrier = pltpu.get_barrier_semaphore()
    for peer in gx_peers:
        pl.semaphore_signal(barrier, inc=1, device_id=(peer, gy), device_id_type=MESH)
    for peer in gy_peers:
        pl.semaphore_signal(barrier, inc=1, device_id=(gx, peer), device_id_type=MESH)

    def gx_copy(src, dst, send, recv, peer):
        return pltpu.make_async_remote_copy(
            src_ref=src, dst_ref=dst, send_sem=send, recv_sem=recv, device_id=(peer, gy), device_id_type=MESH,
        )

    def gy_copy(src, dst, send, recv, peer):
        return pltpu.make_async_remote_copy(
            src_ref=src, dst_ref=dst, send_sem=send, recv_sem=recv, device_id=(gx, peer), device_id_type=MESH,
        )

    def gx_all(lanes, c, arrived, send, recv):
        part = pl.ds(0, LANES - 1)
        return gx_copy(lanes.at[c, part], arrived.at[part], send.at[c], recv.at[c], gx_peers[0])

    def gy_all(lanes, c, arrived, send, recv):
        part = pl.ds(0, LANES - 2)
        return gy_copy(lanes.at[c, part], arrived.at[part], send.at[c], recv.at[c], gy_peers[0])

    own_table(table, counts, z_dest)
    with scope('keys'):
        key_rows = row_keys(blocks_ref[...])
    keys[...] = key_rows.astype(jnp.int32)
    with scope('ldw'):
        loads[0].wait()
    for c in range(CHUNKS):
        group = 256 // STEP
        for first in range(0, LANES, group):
            rows_in = lax.broadcasted_iota(jnp.int32, (STEP, 128), 0) + c * STEP
            wanted = jnp.concatenate(
                [rows_in + table[OWN_BLOCK + first + k] for k in range(group)], axis=0
            )
            picker = jnp.concatenate(
                [jnp.where(wanted == keys[g : g + 1, :], 1.0, 0.0).astype(BF) for g in range(16)], axis=1
            )
            with scope('pack'):
                packed = jnp.dot(picker, feat[...], preferred_element_type=F32).astype(BF)
            lanes_a[c, first : first + group] = packed.reshape(group, STEP, D)
        if c == 0:
            with scope('barr'):
                pl.semaphore_wait(barrier, len(gx_peers) + len(gy_peers))
        for peer in gx_peers:
            gx_copy(lanes_a.at[c, peer], arr_x[c].at[gx], send_a.at[c], recv_a.at[c], peer).start()
        arr_x[c][gx] = lanes_a[c, gx]

    with scope('mov'):
        move_tables(table, z_owner, h_dest, h_back, h_slot)
    padded = jnp.concatenate([key_rows, jnp.zeros((128 - 16, 128), F32)], axis=0)
    turned = padded.T.astype(jnp.int32)
    for g in range(16):
        keys_wide[g * 128 : (g + 1) * 128, :] = jnp.broadcast_to(turned[:, g : g + 1], (128, 128))


    def project(layer, c):
        rows = pl.ds(c * PART, PART)
        values = xs[rows, :].astype(F32)
        normal = normed(values, gain_ref[layer, 0:1, :]).astype(BF)
        joined = jnp.dot(normal, wqkv[layer], preferred_element_type=F32)
        for pair in range(PAIRS):
            q_s[pair, rows, :] = joined[:, pair * 128 : (pair + 1) * 128].astype(BF) * jnp.asarray(0.125, BF)
            k_s[pair, rows, :] = joined[:, D + pair * 128 : D + (pair + 1) * 128].astype(BF)
            v_s[pair, rows, 0:128] = joined[:, 2 * D + pair * 128 : 2 * D + (pair + 1) * 128].astype(BF)
            v_s[pair, rows, 128:256] = jnp.ones((PART, 128), BF)

    def attend(layer, c):
        part = SLOTS * FINE_STEP
        rows = pl.ds(c * part, part)
        low_half = lax.broadcasted_iota(jnp.int32, (part, 128), 1) < 64
        mixed = []
        for pair in range(PAIRS):
            q_pair = q_s[pair, rows, :]
            zero = jnp.zeros_like(q_pair)
            both = jnp.concatenate([jnp.where(low_half, q_pair, zero), jnp.where(low_half, zero, q_pair)], axis=0)
            scores = lax.dot_general(both, k_s[pair], (((1,), (1,)), ((), ())), preferred_element_type=F32)
            highest = jnp.max(scores, axis=-1, keepdims=True)
            weights = jnp.exp(scores - highest).astype(BF)
            summed = jnp.dot(weights, v_s[pair], preferred_element_type=F32)
            chosen = jnp.where(low_half, summed[:part, 0:128], summed[part:, 0:128])
            divisor = jnp.where(low_half, summed[:part, 128:256], summed[part:, 128:256])
            mixed.append((chosen / divisor).astype(BF))
            yield None
        attended = jnp.concatenate(mixed, axis=1)
        yield (xs[rows, :].astype(F32) + jnp.dot(attended, wout[layer], preferred_element_type=F32)).astype(BF)

    def feed_forward(layer, after):
        middle = after.astype(F32)
        normal = normed(middle, gain_ref[layer, 1:2, :]).astype(BF)
        total = middle
        for j in range(4):
            cols = slice(j * 512, (j + 1) * 512)
            hidden = gelu(jnp.dot(normal, wup[layer, :, cols], preferred_element_type=F32)).astype(BF)
            total = total + jnp.dot(hidden, wdown[layer, cols, :], preferred_element_type=F32)
            yield None
        yield total.astype(BF).reshape(SLOTS, FINE_STEP, D)

    def receive_and_project(layer, waits, block_of):
        def body(c, carry):
            for i in range(CHUNKS):
                @pl.when(c == i)
                def _():
                    with scope('wait'):
                        waits(i)
                    for slot in range(SLOTS):
                        for j, piece in enumerate(block_of(i, slot)):
                            at = i * PART + j * SLOTS * FINE_STEP + slot * FINE_STEP
                            xs[at : at + FINE_STEP, :] = piece
            with scope('proj'):
                project(layer, c)
            return carry
        lax.fori_loop(0, CHUNKS, body, 0)

    fold = FINE // CHUNKS

    def wait_x(i):
        gx_all(lanes_a, i, arr_x[i], send_a, recv_a).wait_recv()

    def block_x(i, slot):
        block = arr_x[i][table[FROM_LANE + slot]]
        return [block[j * FINE_STEP : (j + 1) * FINE_STEP, :] for j in range(fold)]

    def wait_1(i):
        for j in range(i * fold, i * fold + fold):
            gy_all(lanes_1, j, arr_1[j], send_1, recv_1).wait_recv()

    def block_1(i, slot):
        return [arr_1[j][table[RECV_LANE + slot]] for j in range(i * fold, i * fold + fold)]

    def forward(i):
        with scope('waitG2'):
            gy_all(lanes_2, i, arr_2[i], send_2, recv_2).wait_recv()
        for k in range(LANES):
            lanes_b[i, k] = arr_2[i][table[HOME_LANE + k]]
        for peer in gx_peers:
            gx_copy(lanes_b.at[i, peer], arr_b.at[i, gx], send_b.at[i], recv_b.at[i], peer).start()
        arr_b[i, gx] = lanes_b[i, gx]

    def compute_and_send(layer, first, lanes, arrived, send, recv, meanwhile):
        def deliver(i):
            for peer in gy_peers:
                pair = pl.ds(peer * 2, 2)
                gy_copy(lanes.at[i, pair], arrived[i].at[pl.ds(gy * 2, 2)], send.at[i], recv.at[i], peer).start()
            for p in range(2):
                arrived[i][gy * 2 + p] = lanes[i, gy * 2 + p]

        def fill(c):
            for lane in range(LANES):
                lanes[c, lane] = y_s[table[first + lane]]

        with scope('att'):
            mid_s[...] = list(attend(layer, 0))[-1]

        def body(c, carry):
            with scope('both'):
                lower = feed_forward(layer, mid_s[...])
                for upper in attend(layer, c + 1):
                    done = next(lower)
                mid_s[...] = upper
                y_s[...] = done
            fill(c)
            for i in range(FINE - 1):
                @pl.when(c == i)
                def _():
                    deliver(i)
                    if meanwhile is not None and i >= 2:
                        meanwhile(i - 2)
            return carry
        lax.fori_loop(0, FINE - 1, body, 0)
        with scope('mlp'):
            y_s[...] = list(feed_forward(layer, mid_s[...]))[-1]
        fill(FINE - 1)
        deliver(FINE - 1)

    loads[1].wait()
    receive_and_project(0, wait_x, block_x)
    for load in loads[2:5]:
        load.wait()
    compute_and_send(0, SEND_SLOT, lanes_1, arr_1, send_1, recv_1, None)
    loads[5].wait()
    receive_and_project(1, wait_1, block_1)
    for load in loads[6:]:
        load.wait()
    compute_and_send(1, BACK_SLOT, lanes_2, arr_2, send_2, recv_2, forward)

    quarter = lax.broadcasted_iota(jnp.int32, (1, 128), 1)

    def unpack(c, carry):
        with scope('waitB'):
            for j in range(fold):
                i = c * fold + j
                gx_all(lanes_b, i, arr_b.at[i], send_b, recv_b).wait_recv()
        wanted = []
        count = 128 // FINE_STEP
        for j in range(fold):
            shift = (c * fold + j) * FINE_STEP
            for first in range(0, LANES, count):
                chosen = jnp.full((1, 128), table[OWN_BLOCK + first] + shift, jnp.int32)
                for k in range(1, count):
                    lane_key = table[OWN_BLOCK + first + k] + shift - k * FINE_STEP
                    chosen = jnp.where(quarter < k * FINE_STEP, chosen, lane_key)
                wanted.append(chosen + quarter)
        landed = arr_b[pl.ds(c * fold, fold)].reshape(fold * LANES * FINE_STEP, D)
        for tile in range(4):
            rows = slice(tile * 512, (tile + 1) * 512)
            wide = keys_wide[rows, :]
            picker = jnp.concatenate([jnp.where(wide == w, 1.0, 0.0).astype(BF) for w in wanted], axis=1)
            with scope('unp'):
                part = jnp.dot(picker, landed, preferred_element_type=F32).astype(BF)
            if isinstance(c, int):
                out_ref[rows, :] = part
            else:
                out_ref[rows, :] = out_ref[rows, :] + part
        return carry

    forward(FINE - 3)
    forward(FINE - 2)
    unpack(0, 0)
    forward(FINE - 1)
    lax.fori_loop(1, CHUNKS, unpack, 0)

    for c in range(CHUNKS):
        gx_all(lanes_a, c, arr_x[c], send_a, recv_a).wait_send()
    for c in range(FINE):
        gy_all(lanes_1, c, arr_1[c], send_1, recv_1).wait_send()
        gy_all(lanes_2, c, arr_2[c], send_2, recv_2).wait_send()
        gx_all(lanes_b, c, arr_b.at[c], send_b, recv_b).wait_send()


def shards(
    features, point_block, block_count, z_dest_dev, z_dest_slot, z_back_owner, z_back_block,
    hil_dest_dev, hil_dest_slot, hil_back_dev, hil_back_slot, norm_gain, w_qkv, w_out, w_up, w_down,
):
    any_space = pl.BlockSpec(memory_space=pl.ANY)
    vmem = pl.BlockSpec(memory_space=pltpu.VMEM)
    dma = pltpu.SemaphoreType.DMA
    landing = [pltpu.VMEM((LANES, STEP, D), BF) for _ in range(CHUNKS)]
    landing += [pltpu.VMEM((LANES, FINE_STEP, D), BF) for _ in range(2 * FINE)]
    return pl.pallas_call(
        kernel,
        out_shape=jax.ShapeDtypeStruct((ROWS, D), BF),
        in_specs=[pl.BlockSpec(memory_space=pltpu.SMEM)] * 6 + [vmem, vmem] + [any_space] * 5,
        out_specs=vmem,
        scratch_shapes=[
            pltpu.SMEM((80,), jnp.int32),
            pltpu.VMEM((ROWS, D), BF),
            pltpu.VMEM((2, D, 3 * D), BF),
            pltpu.VMEM((2, D, D), BF),
            pltpu.VMEM((2, D, FF), BF),
            pltpu.VMEM((2, FF, D), BF),
            pltpu.VMEM((16, 128), jnp.int32),
            pltpu.VMEM((CHUNKS, LANES, STEP, D), BF),
            pltpu.VMEM((ROWS, 128), jnp.int32),
            pltpu.VMEM((SLOTS * BLOCK, D), BF),
            pltpu.VMEM((PAIRS, SLOTS * BLOCK, 128), BF),
            pltpu.VMEM((PAIRS, SLOTS * BLOCK, 128), BF),
            pltpu.VMEM((PAIRS, SLOTS * BLOCK, 256), BF),
            pltpu.VMEM((SLOTS * FINE_STEP, D), BF),
            pltpu.VMEM((SLOTS, FINE_STEP, D), BF),
            pltpu.VMEM((FINE, LANES, FINE_STEP, D), BF),
            pltpu.VMEM((FINE, LANES, FINE_STEP, D), BF),
            pltpu.VMEM((FINE, LANES, FINE_STEP, D), BF),
            pltpu.VMEM((FINE, LANES, FINE_STEP, D), BF),
        ]
        + landing
        + [
            dma((9,)),
            dma((CHUNKS,)), dma((CHUNKS,)), dma((FINE,)), dma((FINE,)),
            dma((FINE,)), dma((FINE,)), dma((FINE,)), dma((FINE,)),
        ],
        compiler_params=pltpu.CompilerParams(
            collective_id=0, has_side_effects=True, vmem_limit_bytes=63 * 1024 * 1024
        ),
    )(
        block_count, z_dest_dev, z_back_owner, hil_dest_dev, hil_back_dev, hil_back_slot,
        point_block.reshape(16, 128), norm_gain, features, w_qkv, w_out, w_up, w_down,
    )


def solution(mesh):
    split = P(("gx", "gy"), None)
    flat = P(("gx", "gy"))
    in_specs = (split, flat, flat) + (split,) * 8 + (P(),) * 5
    return jax.shard_map(shards, mesh=mesh, in_specs=in_specs, out_specs=split, check_vma=False)
```

time: 125 us -> 110 us (0.88)
  Pallas kernels: 114 us -> 106 us
  other arithmetic: 5.34 us -> 0 us
  local copies, waits for them, and re-layouts: 4.3 us -> 3.05 us
    pallas_call x1, Pallas kernels: 114 us -> 106 us  [shards(): pl.pallas_call(kernel, out_shape=jax.ShapeDtypeStruct((ROWS, D), BF), in_...]
    reduce_sum x4 -> x0, other arithmetic: 2.69 us -> none  [the longest x2 1.83 us: rank_within(): return jnp.sum((same & before).astype(jnp.int32), axis=1)]
    eq x3 -> x0, other arithmetic: 1.98 us -> none  [placed(): hit = keys[None, :] == lanes[:, None]]
    concatenate x1 -> x0, local copies, waits for them, and re-layouts: 1.25 us -> none  [shards(): jnp.concatenate([placed(send_keys, slots), recv_keys, placed(recv_keys, s...]
where the time goes in v2:
time: 110 us; the launch traced here: 109 us
  Pallas kernels  106 us (96%)
  local copies, waits for them, and re-layouts  3.05 us (3%)
    pallas_call x1, Pallas kernels, shards(): pl.pallas_call(kernel, out_shape=jax.ShapeDtypeStruct((ROWS, D), BF), in_...  106 us
    unnamed x1, local copies, waits for them, and re-layouts  3.05 us

profile of v2, /device:TPU:1, one launch (start us, length us, event | category | flops | bytes accessed | tf_op | source)
XLA Modules:
  0.0 109.4 jit_solution(515138174330974421)
XLA Ops:
  0.7 105.7 %shard_map.127 = bf16[2048,512]{1,0:T(8,128)(2,1)} custom-call(s32[1]{0:T(128)S(6)} %copy.15.counts, s32[1,16]{1,0:T(1,128)} %z_dest.1, s32[1,8]{1,0:T(1,128)} %z_owner.1, s32[1,8]{1,0:T(1,128)} %h_dest.1, s32[1,8]{1,0:T(1,128)} %h_back.1, s32[1,8]{1,0:T(1,128)} %h_slot.1, s32[16,128]{1,0:T(8,128)} %bitcast.1, f32[2,2,512]{2,1,0:T(2,128)} %gain_ref.1, ...), custom_call_target="tpu_custom_call" | custom-call | tf_op jit(solution)/shard_map/pallas_call | solution.py:381
  106.4 3.0 %copy.16 = bf16[2048,512]{1,0:T(8,128)(2,1)} copy(bf16[2048,512]{1,0:T(8,128)(2,1)} %shard_map.127) | data formatting | bytes 4194304

commit v3 on v2

--- a/solution.py
+++ b/solution.py
@@ -75,7 +75,8 @@
 
 
 def own_table(table, counts, z_dest):
-    dests = [jnp.where(b < counts[0], z_dest[0, b], -1) for b in range(CAP)]
+    live = counts[0]
+    dests = [jnp.where(b < live, z_dest[0, b], -1) for b in range(CAP)]
     for lane in range(LANES):
         chosen = jnp.int32(NOWHERE)
         for b in range(CAP):
@@ -116,9 +117,10 @@
 
 
 def kernel(
-    counts, z_dest, z_owner, h_dest, h_back, h_slot,
-    blocks_ref, gain_ref, feat_h, wqkv_h, wout_h, wup_h, wdown_h, out_ref,
-    table, feat, wqkv, wout, wup, wdown, keys, lanes_a, keys_wide, xs, q_s, k_s, v_s, mid_s, y_s, lanes_1, lanes_2, lanes_b, arr_b,
+    counts, z_dest_h, z_owner_h, h_dest_h, h_back_h, h_slot_h, blocks_h, gain_h,
+    feat_h, wqkv_h, wout_h, wup_h, wdown_h, out_ref,
+    z_dest, z_owner, h_dest, h_back, h_slot, blocks_ref, gain_ref,
+    table, feat, wqkv, wout, wup, wdown, keys, lanes_a, keys_wide, pick_s, xs, q_s, k_s, v_s, mid_s, y_s, lanes_1, lanes_2, lanes_b, arr_b,
     *rest,
 ):
     arr_x, arr_1, arr_2 = rest[:CHUNKS], rest[CHUNKS : CHUNKS + FINE], rest[CHUNKS + FINE : CHUNKS + 2 * FINE]
@@ -130,6 +132,22 @@
     gx_peers = [((z + dz) % 4) * 4 + (y + dy) % 4 for dz, dy in GX_OFFSETS]
     gy_peers = [((x + dx) % 4) * 2 + (core + dc) % 2 for dx, dc in GY_OFFSETS]
 
+    barrier = pltpu.get_barrier_semaphore()
+    for peer in gx_peers:
+        pl.semaphore_signal(barrier, inc=1, device_id=(peer, gy), device_id_type=MESH)
+    for peer in gy_peers:
+        pl.semaphore_signal(barrier, inc=1, device_id=(gx, peer), device_id_type=MESH)
+
+    small = []
+    for i, (src, dst) in enumerate(
+        (
+            (blocks_h, blocks_ref), (z_dest_h, z_dest), (z_owner_h, z_owner),
+            (h_dest_h, h_dest), (h_back_h, h_back), (h_slot_h, h_slot), (gain_h, gain_ref),
+        )
+    ):
+        small.append(pltpu.make_async_copy(src, dst, local_sem.at[9 + i]))
+    for load in small:
+        load.start()
     loads = [pltpu.make_async_copy(feat_h, feat, local_sem.at[0])]
     for layer in range(2):
         for i, (src, dst) in enumerate(((wqkv_h, wqkv), (wout_h, wout), (wup_h, wup), (wdown_h, wdown))):
@@ -137,12 +155,6 @@
     for load in loads:
         load.start()
 
-    barrier = pltpu.get_barrier_semaphore()
-    for peer in gx_peers:
-        pl.semaphore_signal(barrier, inc=1, device_id=(peer, gy), device_id_type=MESH)
-    for peer in gy_peers:
-        pl.semaphore_signal(barrier, inc=1, device_id=(gx, peer), device_id_type=MESH)
-
     def gx_copy(src, dst, send, recv, peer):
         return pltpu.make_async_remote_copy(
             src_ref=src, dst_ref=dst, send_sem=send, recv_sem=recv, device_id=(peer, gy), device_id_type=MESH,
@@ -161,18 +173,21 @@
         part = pl.ds(0, LANES - 2)
         return gy_copy(lanes.at[c, part], arrived.at[part], send.at[c], recv.at[c], gy_peers[0])
 
+    for load in small[:2]:
+        load.wait()
     own_table(table, counts, z_dest)
     with scope('keys'):
         key_rows = row_keys(blocks_ref[...])
     keys[...] = key_rows.astype(jnp.int32)
     with scope('ldw'):
         loads[0].wait()
+    order = gx_peers + [gx]
     for c in range(CHUNKS):
         group = 256 // STEP
         for first in range(0, LANES, group):
             rows_in = lax.broadcasted_iota(jnp.int32, (STEP, 128), 0) + c * STEP
             wanted = jnp.concatenate(
-                [rows_in + table[OWN_BLOCK + first + k] for k in range(group)], axis=0
+                [rows_in + table[OWN_BLOCK + order[first + k]] for k in range(group)], axis=0
             )
             picker = jnp.concatenate(
                 [jnp.where(wanted == keys[g : g + 1, :], 1.0, 0.0).astype(BF) for g in range(16)], axis=1
@@ -180,13 +195,15 @@
             with scope('pack'):
                 packed = jnp.dot(picker, feat[...], preferred_element_type=F32).astype(BF)
             lanes_a[c, first : first + group] = packed.reshape(group, STEP, D)
-        if c == 0:
-            with scope('barr'):
-                pl.semaphore_wait(barrier, len(gx_peers) + len(gy_peers))
-        for peer in gx_peers:
-            gx_copy(lanes_a.at[c, peer], arr_x[c].at[gx], send_a.at[c], recv_a.at[c], peer).start()
-        arr_x[c][gx] = lanes_a[c, gx]
-
+            if c == 0 and first == 0:
+                with scope('barr'):
+                    pl.semaphore_wait(barrier, len(gx_peers) + len(gy_peers))
+            for k in range(first, min(first + group, LANES - 1)):
+                gx_copy(lanes_a.at[c, k], arr_x[c].at[gx], send_a.at[c], recv_a.at[c], order[k]).start()
+        arr_x[c][gx] = lanes_a[c, LANES - 1]
+
+    for load in small[2:]:
+        load.wait()
     with scope('mov'):
         move_tables(table, z_owner, h_dest, h_back, h_slot)
     padded = jnp.concatenate([key_rows, jnp.zeros((128 - 16, 128), F32)], axis=0)
@@ -194,6 +211,8 @@
     for g in range(16):
         keys_wide[g * 128 : (g + 1) * 128, :] = jnp.broadcast_to(turned[:, g : g + 1], (128, 128))
 
+
+    fold = FINE // CHUNKS
 
     def project(layer, c):
         rows = pl.ds(c * PART, PART)
@@ -237,8 +256,26 @@
             yield None
         yield total.astype(BF).reshape(SLOTS, FINE_STEP, D)
 
+    quarter = lax.broadcasted_iota(jnp.int32, (1, 128), 1)
+
+    def pickers(c):
+        count = 128 // FINE_STEP
+        for j in range(fold):
+            shift = (c * fold + j) * FINE_STEP
+            for first in range(0, LANES, count):
+                chosen = jnp.full((1, 128), table[OWN_BLOCK + first] + shift, jnp.int32)
+                for k in range(1, count):
+                    lane_key = table[OWN_BLOCK + first + k] + shift - k * FINE_STEP
+                    chosen = jnp.where(quarter < k * FINE_STEP, chosen, lane_key)
+                at = first * FINE_STEP
+                hit = keys_wide[...] == chosen + quarter
+                pick_s[c * fold + j, :, at : at + 128] = jnp.where(hit, 1.0, 0.0).astype(BF)
+
     def receive_and_project(layer, waits, block_of):
         def body(c, carry):
+            if layer == 0:
+                with scope('pick'):
+                    pickers(c)
             for i in range(CHUNKS):
                 @pl.when(c == i)
                 def _():
@@ -253,7 +290,6 @@
             return carry
         lax.fori_loop(0, CHUNKS, body, 0)
 
-    fold = FINE // CHUNKS
 
     def wait_x(i):
         gx_all(lanes_a, i, arr_x[i], send_a, recv_a).wait_recv()
@@ -325,41 +361,31 @@
         load.wait()
     compute_and_send(1, BACK_SLOT, lanes_2, arr_2, send_2, recv_2, forward)
 
-    quarter = lax.broadcasted_iota(jnp.int32, (1, 128), 1)
-
-    def unpack(c, carry):
+    def unpack(*pieces):
         with scope('waitB'):
-            for j in range(fold):
-                i = c * fold + j
+            for i in pieces:
                 gx_all(lanes_b, i, arr_b.at[i], send_b, recv_b).wait_recv()
-        wanted = []
-        count = 128 // FINE_STEP
-        for j in range(fold):
-            shift = (c * fold + j) * FINE_STEP
-            for first in range(0, LANES, count):
-                chosen = jnp.full((1, 128), table[OWN_BLOCK + first] + shift, jnp.int32)
-                for k in range(1, count):
-                    lane_key = table[OWN_BLOCK + first + k] + shift - k * FINE_STEP
-                    chosen = jnp.where(quarter < k * FINE_STEP, chosen, lane_key)
-                wanted.append(chosen + quarter)
-        landed = arr_b[pl.ds(c * fold, fold)].reshape(fold * LANES * FINE_STEP, D)
         for tile in range(4):
             rows = slice(tile * 512, (tile + 1) * 512)
-            wide = keys_wide[rows, :]
-            picker = jnp.concatenate([jnp.where(wide == w, 1.0, 0.0).astype(BF) for w in wanted], axis=1)
-            with scope('unp'):
-                part = jnp.dot(picker, landed, preferred_element_type=F32).astype(BF)
-            if isinstance(c, int):
-                out_ref[rows, :] = part
+            part = None
+            for i in pieces:
+                landed = arr_b[i].reshape(LANES * FINE_STEP, D)
+                with scope('unp'):
+                    piece = jnp.dot(pick_s[i, rows, :], landed, preferred_element_type=F32)
+                part = piece if part is None else part + piece
+            if pieces[0] == 0:
+                out_ref[rows, :] = part.astype(BF)
             else:
-                out_ref[rows, :] = out_ref[rows, :] + part
-        return carry
+                out_ref[rows, :] = out_ref[rows, :] + part.astype(BF)
 
     forward(FINE - 3)
     forward(FINE - 2)
-    unpack(0, 0)
+    unpack(0, 1)
     forward(FINE - 1)
-    lax.fori_loop(1, CHUNKS, unpack, 0)
+    unpack(2, 3)
+    unpack(4, 5)
+    unpack(6)
+    unpack(7)
 
     for c in range(CHUNKS):
         gx_all(lanes_a, c, arr_x[c], send_a, recv_a).wait_send()
@@ -373,17 +399,23 @@
     features, point_block, block_count, z_dest_dev, z_dest_slot, z_back_owner, z_back_block,
     hil_dest_dev, hil_dest_slot, hil_back_dev, hil_back_slot, norm_gain, w_qkv, w_out, w_up, w_down,
 ):
-    any_space = pl.BlockSpec(memory_space=pl.ANY)
     vmem = pl.BlockSpec(memory_space=pltpu.VMEM)
     dma = pltpu.SemaphoreType.DMA
     landing = [pltpu.VMEM((LANES, STEP, D), BF) for _ in range(CHUNKS)]
     landing += [pltpu.VMEM((LANES, FINE_STEP, D), BF) for _ in range(2 * FINE)]
     return pl.pallas_call(
         kernel,
-        out_shape=jax.ShapeDtypeStruct((ROWS, D), BF),
-        in_specs=[pl.BlockSpec(memory_space=pltpu.SMEM)] * 6 + [vmem, vmem] + [any_space] * 5,
+        out_shape=pltpu.VMEM((ROWS, D), BF),
+        in_specs=[pl.BlockSpec(memory_space=pltpu.SMEM)] + [pl.BlockSpec(memory_space=pltpu.HBM)] * 12,
         out_specs=vmem,
         scratch_shapes=[
+            pltpu.SMEM((1, CAP), jnp.int32),
+            pltpu.SMEM((1, SLOTS), jnp.int32),
+            pltpu.SMEM((1, SLOTS), jnp.int32),
+            pltpu.SMEM((1, SLOTS), jnp.int32),
+            pltpu.SMEM((1, SLOTS), jnp.int32),
+            pltpu.VMEM((16, 128), jnp.int32),
+            pltpu.VMEM((2, 2, D), F32),
             pltpu.SMEM((80,), jnp.int32),
             pltpu.VMEM((ROWS, D), BF),
             pltpu.VMEM((2, D, 3 * D), BF),
@@ -393,6 +425,7 @@
             pltpu.VMEM((16, 128), jnp.int32),
             pltpu.VMEM((CHUNKS, LANES, STEP, D), BF),
             pltpu.VMEM((ROWS, 128), jnp.int32),
+            pltpu.VMEM((FINE, ROWS, LANES * FINE_STEP), BF),
             pltpu.VMEM((SLOTS * BLOCK, D), BF),
             pltpu.VMEM((PAIRS, SLOTS * BLOCK, 128), BF),
             pltpu.VMEM((PAIRS, SLOTS * BLOCK, 128), BF),
@@ -406,16 +439,22 @@
         ]
         + landing
         + [
-            dma((9,)),
+            dma((16,)),
             dma((CHUNKS,)), dma((CHUNKS,)), dma((FINE,)), dma((FINE,)),
             dma((FINE,)), dma((FINE,)), dma((FINE,)), dma((FINE,)),
         ],
         compiler_params=pltpu.CompilerParams(
-            collective_id=0, has_side_effects=True, vmem_limit_bytes=63 * 1024 * 1024
+            collective_id=0, has_side_effects=True, vmem_limit_bytes=56 * 1024 * 1024
         ),
     )(
-        block_count, z_dest_dev, z_back_owner, hil_dest_dev, hil_back_dev, hil_back_slot,
-        point_block.reshape(16, 128), norm_gain, features, w_qkv, w_out, w_up, w_down,
+        block_count,
+        *[
+            pltpu.with_memory_space_constraint(array, pltpu.HBM)
+            for array in (
+                z_dest_dev, z_back_owner, hil_dest_dev, hil_back_dev, hil_back_slot,
+                point_block.reshape(16, 128), norm_gain, features, w_qkv, w_out, w_up, w_down,
+            )
+        ]
     )
 
 

time: 110 us -> 105 us (0.955)
  Pallas kernels: 106 us -> 103 us
  local copies, waits for them, and re-layouts: 3.05 us -> 1.32 us
    pallas_call x1, Pallas kernels: 106 us -> 103 us  [shards(): pl.pallas_call(kernel, out_shape=pltpu.VMEM((ROWS, D), BF), in_specs=[pl....]
    unnamed x1, local copies, waits for them, and re-layouts: 3.05 us -> 1.32 us
where the time goes in v3:
time: 105 us
  Pallas kernels  103 us (98%)
  local copies, waits for them, and re-layouts  1.32 us (1%)
    pallas_call x1, Pallas kernels, shards(): pl.pallas_call(kernel, out_shape=pltpu.VMEM((ROWS, D), BF), in_specs=[pl....  103 us

profile of v3, /device:TPU:1, one launch (start us, length us, event | category | flops | bytes accessed | tf_op | source)
XLA Modules:
  0.0 105.1 jit_solution(17936193077692005179)
XLA Ops:
  0.7 103.1 %shard_map.127 = bf16[2048,512]{1,0:T(8,128)(2,1)S(1)} custom-call(s32[1]{0:T(128)S(6)} %copy.16.counts, s32[1,16]{1,0:T(1,128)} %z_dest_h.1, s32[1,8]{1,0:T(1,128)} %z_owner_h.1, s32[1,8]{1,0:T(1,128)} %h_dest_h.1, s32[1,8]{1,0:T(1,128)} %h_back_h.1, s32[1,8]{1,0:T(1,128)} %h_slot_h.1, s32[16,128]{1,0:T(8,128)} %bitcast.1, f32[2,2,512]{2,1,0:T(2,128)} %gain_h.1, ...), custom_call_target="tpu_custom_call" | custom-call | tf_op jit(solution)/shard_map/pallas_call | solution.py:406
  103.8 1.3 %copy.15 = bf16[2048,512]{1,0:T(8,128)(2,1)} copy(bf16[2048,512]{1,0:T(8,128)(2,1)S(1)} %shard_map.127) | data formatting | bytes 4194304

commit v4 on v3

--- a/solution.py
+++ b/solution.py
@@ -25,6 +25,8 @@
 PART = SLOTS * STEP
 FINE = 8
 FINE_STEP = BLOCK // FINE
+EARLY = 2
+EARLY_KEYS = SLOTS * (BLOCK - STEP)
 LANES = 16
 PAIRS = 4
 EPSILON = 1e-05
@@ -120,7 +122,7 @@
     counts, z_dest_h, z_owner_h, h_dest_h, h_back_h, h_slot_h, blocks_h, gain_h,
     feat_h, wqkv_h, wout_h, wup_h, wdown_h, out_ref,
     z_dest, z_owner, h_dest, h_back, h_slot, blocks_ref, gain_ref,
-    table, feat, wqkv, wout, wup, wdown, keys, lanes_a, keys_wide, pick_s, xs, q_s, k_s, v_s, mid_s, y_s, lanes_1, lanes_2, lanes_b, arr_b,
+    table, feat, wqkv, wout, wup, wdown, keys, lanes_a, keys_wide, pick_s, xs, q_s, k_s, v_s, early_sum, early_max, mid_s, y_s, lanes_1, lanes_2, lanes_b, arr_b,
     *rest,
 ):
     arr_x, arr_1, arr_2 = rest[:CHUNKS], rest[CHUNKS : CHUNKS + FINE], rest[CHUNKS + FINE : CHUNKS + 2 * FINE]
@@ -225,19 +227,44 @@
             v_s[pair, rows, 0:128] = joined[:, 2 * D + pair * 128 : 2 * D + (pair + 1) * 128].astype(BF)
             v_s[pair, rows, 128:256] = jnp.ones((PART, 128), BF)
 
-    def attend(layer, c):
-        part = SLOTS * FINE_STEP
+    part = SLOTS * FINE_STEP
+    low_half = lax.broadcasted_iota(jnp.int32, (part, 128), 1) < 64
+
+    def both_heads(c, pair):
+        q_pair = q_s[pair, pl.ds(c * part, part), :]
+        zero = jnp.zeros_like(q_pair)
+        return jnp.concatenate([jnp.where(low_half, q_pair, zero), jnp.where(low_half, zero, q_pair)], axis=0)
+
+    def against(queries, pair, keys_of):
+        return lax.dot_general(
+            queries, k_s[pair, keys_of, :], (((1,), (1,)), ((), ())), preferred_element_type=F32
+        )
+
+    def attend_early(c):
+        keys_of = slice(0, EARLY_KEYS)
+        for pair in range(PAIRS):
+            scores = against(both_heads(c, pair), pair, keys_of)
+            highest = jnp.max(scores, axis=-1, keepdims=True)
+            weights = jnp.exp(scores - highest).astype(BF)
+            early_sum[c, pair] = jnp.dot(weights, v_s[pair, keys_of, :], preferred_element_type=F32)
+            early_max[c, pair] = jnp.broadcast_to(highest, (2 * part, 128))
+
+    def attend(layer, c, early=False):
+        keys_of = slice(EARLY_KEYS if early else 0, SLOTS * BLOCK)
         rows = pl.ds(c * part, part)
-        low_half = lax.broadcasted_iota(jnp.int32, (part, 128), 1) < 64
         mixed = []
         for pair in range(PAIRS):
-            q_pair = q_s[pair, rows, :]
-            zero = jnp.zeros_like(q_pair)
-            both = jnp.concatenate([jnp.where(low_half, q_pair, zero), jnp.where(low_half, zero, q_pair)], axis=0)
-            scores = lax.dot_general(both, k_s[pair], (((1,), (1,)), ((), ())), preferred_element_type=F32)
+            scores = against(both_heads(c, pair), pair, keys_of)
             highest = jnp.max(scores, axis=-1, keepdims=True)
+            if early:
+                before = early_max[c, pair]
+                wide = jnp.maximum(jnp.broadcast_to(highest, before.shape), before)
+                highest = jnp.concatenate([wide, wide], axis=1)
             weights = jnp.exp(scores - highest).astype(BF)
-            summed = jnp.dot(weights, v_s[pair], preferred_element_type=F32)
+            summed = jnp.dot(weights, v_s[pair, keys_of, :], preferred_element_type=F32)
+            if early:
+                kept = jnp.exp(before - wide)
+                summed = summed + early_sum[c, pair] * jnp.concatenate([kept, kept], axis=1)
             chosen = jnp.where(low_half, summed[:part, 0:128], summed[part:, 0:128])
             divisor = jnp.where(low_half, summed[:part, 128:256], summed[part:, 128:256])
             mixed.append((chosen / divisor).astype(BF))
@@ -276,6 +303,13 @@
             if layer == 0:
                 with scope('pick'):
                     pickers(c)
+
+            @pl.when(c == CHUNKS - 1)
+            def _():
+                with scope('early'):
+                    for e in range(EARLY):
+                        attend_early(e)
+
             for i in range(CHUNKS):
                 @pl.when(c == i)
                 def _():
@@ -326,25 +360,32 @@
             for lane in range(LANES):
                 lanes[c, lane] = y_s[table[first + lane]]
 
-        with scope('att'):
-            mid_s[...] = list(attend(layer, 0))[-1]
-
-        def body(c, carry):
+        def send_off(i):
+            deliver(i)
+            if meanwhile is not None and i >= 2:
+                meanwhile(i - 2)
+
+        def merged(c, early):
             with scope('both'):
                 lower = feed_forward(layer, mid_s[...])
-                for upper in attend(layer, c + 1):
+                for upper in attend(layer, c + 1, early):
                     done = next(lower)
                 mid_s[...] = upper
                 y_s[...] = done
             fill(c)
-            for i in range(FINE - 1):
-                @pl.when(c == i)
-                def _():
-                    deliver(i)
-                    if meanwhile is not None and i >= 2:
-                        meanwhile(i - 2)
+
+        def body(c, carry):
+            merged(c, False)
+            for i in range(EARLY - 1, FINE - 1):
+                pl.when(c == i)(lambda i=i: send_off(i))
             return carry
-        lax.fori_loop(0, FINE - 1, body, 0)
+
+        with scope('att'):
+            mid_s[...] = list(attend(layer, 0, True))[-1]
+        for c in range(EARLY - 1):
+            merged(c, True)
+            send_off(c)
+        lax.fori_loop(EARLY - 1, FINE - 1, body, 0)
         with scope('mlp'):
             y_s[...] = list(feed_forward(layer, mid_s[...]))[-1]
         fill(FINE - 1)
@@ -430,6 +471,8 @@
             pltpu.VMEM((PAIRS, SLOTS * BLOCK, 128), BF),
             pltpu.VMEM((PAIRS, SLOTS * BLOCK, 128), BF),
             pltpu.VMEM((PAIRS, SLOTS * BLOCK, 256), BF),
+            pltpu.VMEM((EARLY, PAIRS, 2 * SLOTS * FINE_STEP, 256), F32),
+            pltpu.VMEM((EARLY, PAIRS, 2 * SLOTS * FINE_STEP, 128), F32),
             pltpu.VMEM((SLOTS * FINE_STEP, D), BF),
             pltpu.VMEM((SLOTS, FINE_STEP, D), BF),
             pltpu.VMEM((FINE, LANES, FINE_STEP, D), BF),

time: 105 us -> 102 us (0.971)
  Pallas kernels: 103 us -> 100 us
    pallas_call x1, Pallas kernels: 103 us -> 100 us  [shards(): pl.pallas_call(kernel, out_shape=pltpu.VMEM((ROWS, D), BF), in_specs=[pl....]
where the time goes in v4:
time: 102 us
  Pallas kernels  100 us (98%)
  local copies, waits for them, and re-layouts  1.32 us (1%)
    pallas_call x1, Pallas kernels, shards(): pl.pallas_call(kernel, out_shape=pltpu.VMEM((ROWS, D), BF), in_specs=[pl....  100 us

profile of v4, /device:TPU:1, one launch (start us, length us, event | category | flops | bytes accessed | tf_op | source)
XLA Modules:
  0.0 102.3 jit_solution(8894028566309567037)
XLA Ops:
  0.7 100.3 %shard_map.127 = bf16[2048,512]{1,0:T(8,128)(2,1)S(1)} custom-call(s32[1]{0:T(128)S(6)} %copy.16.counts, s32[1,16]{1,0:T(1,128)} %z_dest_h.1, s32[1,8]{1,0:T(1,128)} %z_owner_h.1, s32[1,8]{1,0:T(1,128)} %h_dest_h.1, s32[1,8]{1,0:T(1,128)} %h_back_h.1, s32[1,8]{1,0:T(1,128)} %h_slot_h.1, s32[16,128]{1,0:T(8,128)} %bitcast.1, f32[2,2,512]{2,1,0:T(2,128)} %gain_h.1, ...), custom_call_target="tpu_custom_call" | custom-call | tf_op jit(solution)/shard_map/pallas_call | solution.py:447
  101.0 1.3 %copy.15 = bf16[2048,512]{1,0:T(8,128)(2,1)} copy(bf16[2048,512]{1,0:T(8,128)(2,1)S(1)} %shard_map.127) | data formatting | bytes 4194304

commit v5 on v4

--- a/solution.py
+++ b/solution.py
@@ -25,7 +25,7 @@
 PART = SLOTS * STEP
 FINE = 8
 FINE_STEP = BLOCK // FINE
-EARLY = 2
+EARLY = 3
 EARLY_KEYS = SLOTS * (BLOCK - STEP)
 LANES = 16
 PAIRS = 4
@@ -365,26 +365,29 @@
             if meanwhile is not None and i >= 2:
                 meanwhile(i - 2)
 
-        def merged(c, early):
+        def merged(c):
             with scope('both'):
                 lower = feed_forward(layer, mid_s[...])
-                for upper in attend(layer, c + 1, early):
+                for upper in attend(layer, c + 1):
                     done = next(lower)
                 mid_s[...] = upper
                 y_s[...] = done
             fill(c)
 
         def body(c, carry):
-            merged(c, False)
+            merged(c)
             for i in range(EARLY - 1, FINE - 1):
                 pl.when(c == i)(lambda i=i: send_off(i))
             return carry
 
+        for c in range(EARLY - 1):
+            with scope('att'):
+                mid_s[...] = list(attend(layer, c, True))[-1]
+                y_s[...] = list(feed_forward(layer, mid_s[...]))[-1]
+            fill(c)
+            send_off(c)
         with scope('att'):
-            mid_s[...] = list(attend(layer, 0, True))[-1]
-        for c in range(EARLY - 1):
-            merged(c, True)
-            send_off(c)
+            mid_s[...] = list(attend(layer, EARLY - 1, True))[-1]
         lax.fori_loop(EARLY - 1, FINE - 1, body, 0)
         with scope('mlp'):
             y_s[...] = list(feed_forward(layer, mid_s[...]))[-1]

time: 102 us -> 101 us (level)
  Pallas kernels: 100 us -> 98.6 us
    pallas_call x1, Pallas kernels: 100 us -> 98.6 us  [shards(): pl.pallas_call(kernel, out_shape=pltpu.VMEM((ROWS, D), BF), in_specs=[pl....]
where the time goes in v5:
time: 101 us
  Pallas kernels  98.6 us (98%)
  local copies, waits for them, and re-layouts  1.32 us (1%)
    pallas_call x1, Pallas kernels, shards(): pl.pallas_call(kernel, out_shape=pltpu.VMEM((ROWS, D), BF), in_specs=[pl....  98.6 us

profile of v5, /device:TPU:1, one launch (start us, length us, event | category | flops | bytes accessed | tf_op | source)
XLA Modules:
  0.0 100.6 jit_solution(18137113681056190386)
XLA Ops:
  0.7 98.6 %shard_map.127 = bf16[2048,512]{1,0:T(8,128)(2,1)S(1)} custom-call(s32[1]{0:T(128)S(6)} %copy.16.counts, s32[1,16]{1,0:T(1,128)} %z_dest_h.1, s32[1,8]{1,0:T(1,128)} %z_owner_h.1, s32[1,8]{1,0:T(1,128)} %h_dest_h.1, s32[1,8]{1,0:T(1,128)} %h_back_h.1, s32[1,8]{1,0:T(1,128)} %h_slot_h.1, s32[16,128]{1,0:T(8,128)} %bitcast.1, f32[2,2,512]{2,1,0:T(2,128)} %gain_h.1, ...), custom_call_target="tpu_custom_call" | custom-call | tf_op jit(solution)/shard_map/pallas_call | solution.py:450
  99.2 1.3 %copy.15 = bf16[2048,512]{1,0:T(8,128)(2,1)} copy(bf16[2048,512]{1,0:T(8,128)(2,1)S(1)} %shard_map.127) | data formatting | bytes 4194304
